TPU v7x, 32 devices: a whole 2x2x4 slice. The times are simulated.
32 devices in a mesh: groups: 2 (over x), genome: 16 (over z, y, core).
Axes of the slice: x: 2, y: 2, z: 4, core: 2. Of those that a mesh axis runs over, the one named last changes fastest.
Arguments:
- factor: bfloat16 [96, 2048, 256], P(('groups', 'genome')), parts along dimension 0, may hold values from -0.5 to 0.5
- normals: bfloat16 [96, 256, 1024], P(('groups', 'genome')), parts along dimension 0, may hold values from -6 to 6
- block_len: int32 [96], P(('groups', 'genome')), parts along dimension 0, may hold values from 256 to 2048, as said below
- block_rank: int32 [96], P(('groups', 'genome')), parts along dimension 0, may hold values from 32 to 256, as said below
- gene_span: int32 [2048, 2], P(('groups', 'genome')), parts along dimension 0, may hold values from 0 to 98304, as said below
- gene_pathways: int32 [2048, 4], P('groups'), parts along dimension 0, may hold values from 0 to 4095, as said below
Outputs:
- pathway_score: float32 [8192, 1024], P(('groups', 'genome')), parts along dimension 0
There are 2 independent parts, one for each index of `groups`. A program takes and returns all parts, laid end to end along the dimension named above; each array names one. Nothing has to cross between parts.
Inputs may be any that keep to these rules, and one draw needn't show every extreme that they name: `block_len`: some block of every draw holds all 2048 slots. `block_rank`: some block of every draw keeps all 256 columns. `gene_span`: genes of rows j * 64 to (j + 1) * 64 - 1 start at a valid slot within slots j * 6144 to (j + 1) * 6144 - 1 and end no later than (j + 1) * 6144 + 2048, never past 98304; the end exceeds the start; some gene of every draw ends exactly 2048 slots past the range of its start. Each gene names 4 different pathways, and every pathway is named by some gene. With q = g * 4 + m, the pathway gene_pathways[g, m] lies in rows r * 256 to (r + 1) * 256 - 1 with r = q % 16, so the genes of one index of genome name at most 16 pathways of one such range, and exactly 16 for some range.
All inputs are finite; a program needn't handle non-finite values.
Results may differ from a plain program's by a relative error of at most 0.0021.
Values may be sent and summed in bfloat16 or wider, within the bound.
No kernel may reach another device: no remote copies, remote signals or barrier semaphores. Data moves between devices by JAX's collectives and lax.ppermute only.
A program may use at most 128 MiB of HBM per device.

v0:
```python
import jax
import jax.numpy as jnp
from jax import lax
from jax.sharding import PartitionSpec as P

PATHWAYS = 4096


def shifted(block, axis, distance):
    devices = range(lax.axis_size(axis))
    route = [(i - distance, i) for i in devices if i - distance in devices]
    return lax.ppermute(block, axis, route)


def covered(positions, spans):
    lower = spans[:, 0][:, None]
    upper = spans[:, 1][:, None]
    return ((positions[None, :] >= lower) & (positions[None, :] < upper)).astype(jnp.float32)


def local(factor, normals, block_len, block_rank, gene_span, gene_pathways):
    block_count, capacity, rank_cap = factor.shape
    sim_count = normals.shape[2]
    local_vars = block_count * capacity
    gene_count = gene_span.shape[0]
    member_count = gene_pathways.shape[1]
    device = lax.axis_index("genome")
    devices_n = lax.axis_size("genome")
    offset = device * local_vars
    kept = jnp.arange(rank_cap, dtype=jnp.int32)[None, :, None] < block_rank[:, None, None]
    trimmed = jnp.where(kept, normals, jnp.zeros_like(normals))
    row_ids = jnp.arange(capacity, dtype=jnp.int32)
    totals = jnp.zeros((gene_count, sim_count), jnp.float32)
    leading = None
    for block in range(block_count):
        coloured = jnp.dot(factor[block], trimmed[block], preferred_element_type=jnp.float32)
        usable = row_ids < block_len[block]
        squares = jnp.where(usable[:, None], coloured * coloured, 0.0)
        positions = offset + block * capacity + row_ids
        totals = totals + jnp.dot(
            covered(positions, gene_span), squares, precision=lax.Precision.HIGHEST
        )
        if block == 0:
            leading = squares
    following = shifted(leading, "genome", -1)
    beyond = offset + local_vars + row_ids
    totals = totals + jnp.dot(
        covered(beyond, gene_span), following, precision=lax.Precision.HIGHEST
    )
    gene_stat = (totals / capacity).astype(jnp.bfloat16)
    path_rows = PATHWAYS // devices_n
    own_ids = device * path_rows + jnp.arange(path_rows, dtype=jnp.int32)
    pair_count = gene_count * member_count
    slot_count = (pair_count + devices_n - 1) // devices_n
    owners = jnp.arange(devices_n, dtype=jnp.int32)[:, None]
    slot_ids = jnp.arange(slot_count, dtype=jnp.int32)[None, :]
    own_shift = device * pair_count % devices_n
    local_pair = (owners - own_shift) % devices_n + slot_ids * devices_n
    valid_send = local_pair < pair_count
    gene_rows = jnp.where(valid_send, local_pair // member_count, 0)
    packed = jnp.where(valid_send[:, :, None], gene_stat[gene_rows], jnp.zeros((), jnp.bfloat16))
    received = lax.all_to_all(packed, "genome", split_axis=0, concat_axis=0, tiled=True)
    sources = jnp.arange(devices_n, dtype=jnp.int32)[:, None]
    source_shift = sources * pair_count % devices_n
    their_pair = (device - source_shift) % devices_n + slot_ids * devices_n
    valid_take = their_pair < pair_count
    global_pair = jnp.where(valid_take, sources * pair_count + their_pair, 0)
    local_path = gene_pathways.reshape(-1)[global_pair] - device * path_rows
    local_path = jnp.where(valid_take, local_path, -1).reshape(-1)
    member = (local_path[None, :] == jnp.arange(path_rows, dtype=jnp.int32)[:, None]).astype(
        jnp.bfloat16
    )
    summed = jnp.dot(
        member,
        received.reshape(devices_n * slot_count, sim_count),
        preferred_element_type=jnp.float32,
    )
    path_count = jnp.sum(
        (gene_pathways.reshape(-1)[None, :] == own_ids[:, None]).astype(jnp.float32), axis=1
    )
    return summed / path_count[:, None]


def solution(mesh):
    in_specs = (
        P(("groups", "genome"), None, None),
        P(("groups", "genome"), None, None),
        P(("groups", "genome")),
        P(("groups", "genome")),
        P(("groups", "genome"), None),
        P("groups", None),
    )
    out_specs = P(("groups", "genome"), None)
    return jax.shard_map(local, mesh=mesh, in_specs=in_specs, out_specs=out_specs, check_vma=False)
```

profile of v0, /device:TPU:0, one launch (start us, length us, event | category | flops | bytes accessed | tf_op | source)
XLA Modules:
  0.0 139.9 jit_solution(4006993111875055616)
XLA Ops:
  0.0 0.7 iota_compare_fusion.5
  0.7 1.4 fusion.67
  2.1 0.7 iota_compare_fusion.4
  2.7 1.6 %broadcast_select_fusion = bf16[3,256,1024]{2,1,0:T(8,128)(2,1)S(1)} fusion(bf16[3,256,1024]{2,1,0:T(8,128)(2,1)} %param.7, pred[3,256]{1,0:T(4,128)(4,1)S(1)} %iota_compare_fusion.5), kind=kLoop, calls=%fused_computation.18 | loop fusion | flops 786432 | bytes 3146496 | tf_op jit(solution)/shard_map/jit(_where)/select_n | solution.py:31
  4.3 2.5 %fusion.22 = f32[1024,2048]{1,0:T(8,128)S(1)} fusion(bf16[3,2048,256]{2,1,0:T(8,128)(2,1)} %param.6, bf16[3,256,1024]{2,1,0:T(8,128)(2,1)S(1)} %broadcast_select_fusion), kind=kOutput, calls=%fused_computation.29 | convolution fusion | flops 1073741824 | bytes 9961472 | tf_op jit(solution)/shard_map/dot_general | solution.py:36
  6.9 4.7 %fusion.6 = f32[2048,1024]{0,1:T(8,128)} fusion(f32[1024,2048]{1,0:T(8,128)S(1)} %fusion.22, pred[2048]{0:T(1024)(128)(4,1)S(1)} %iota_compare_fusion.4), kind=kLoop, calls=%fused_computation.9 | loop fusion | flops 4194304 | bytes 16779264 | tf_op jit(solution)/shard_map/jit(_where)/select_n | solution.py:38
  11.6 1.0 copy-done
  12.6 1.5 %collective-permute-start = (f32[2048,1024]{0,1:T(8,128)}, f32[2048,1024]{0,1:T(8,128)}, u32[]{:S(2)}, u32[]{:S(2)}) collective-permute-start(f32[2048,1024]{0,1:T(8,128)} %fusion.6), channel_id=1, source_target_pairs={{1,0},{2,1},{3,2},{4,3},{5,4},{6,5},{7,6},{8,7},{9,8},{10,9},{11,1... | collective-permute-start | bytes 25165832 | tf_op jit(solution)/shard_map/ppermute | solution.py:12
  14.3 0.6 iota_compare_fusion.2
  14.9 0.6 iota_compare_fusion.3
  15.6 2.5 %fusion.18 = f32[1024,2048]{1,0:T(8,128)S(1)} fusion(bf16[3,2048,256]{2,1,0:T(8,128)(2,1)} %param.6, bf16[3,256,1024]{2,1,0:T(8,128)(2,1)S(1)} %broadcast_select_fusion), kind=kOutput, calls=%fused_computation.25 | convolution fusion | flops 1073741824 | bytes 9961472 | tf_op jit(solution)/shard_map/dot_general | solution.py:36
  18.2 2.5 %fusion.20 = f32[1024,2048]{1,0:T(8,128)S(1)} fusion(bf16[3,2048,256]{2,1,0:T(8,128)(2,1)} %param.6, bf16[3,256,1024]{2,1,0:T(8,128)(2,1)S(1)} %broadcast_select_fusion), kind=kOutput, calls=%fused_computation.27 | convolution fusion | flops 1073741824 | bytes 9961472 | tf_op jit(solution)/shard_map/dot_general | solution.py:36
  20.7 5.0 %fusion = f32[64,1024]{1,0:T(8,128)S(1)} fusion(f32[1024,2048]{1,0:T(8,128)S(1)} %fusion.18, pred[2048]{0:T(1024)(128)(4,1)S(1)} %iota_compare_fusion.2, s32[2048]{0:T(1024)S(1)} %iota_add_fusion.1, s32[64]{0:T(128)S(1)} %get-tuple-element.6, s32[64]{0:T(128)S(1)} %get-tuple-element.5), kind=kOutput, calls=%fused_computation.2 | convolution fusion | flops 1615200256 | bytes 8661504 | tf_op jit(solution)/shard_map/dot_general | solution.py:40
  25.7 5.0 %fusion.3 = f32[64,1024]{1,0:T(8,128)S(1)} fusion(f32[1024,2048]{1,0:T(8,128)S(1)} %fusion.20, pred[2048]{0:T(1024)(128)(4,1)S(1)} %iota_compare_fusion.3, s32[2048]{0:T(1024)S(1)} %iota_add_fusion.2, s32[64]{0:T(128)S(1)} %get-tuple-element.6, s32[64]{0:T(128)S(1)} %get-tuple-element.5), kind=kOutput, calls=%fused_computation.5 | convolution fusion | flops 1615200256 | bytes 8661504 | tf_op jit(solution)/shard_map/dot_general | solution.py:40
  30.7 5.2 %fusion.16 = f32[64,1024]{1,0:T(8,128)S(1)} fusion(f32[64,1024]{1,0:T(8,128)S(1)} %fusion, f32[64,1024]{1,0:T(8,128)S(1)} %fusion.3, f32[1024,2048]{1,0:T(8,128)S(1)} %bitcast.36, pred[2048]{0:T(1024)(128)(4,1)S(1)} %iota_compare_fusion.4, s32[2048]{0:T(1024)S(1)} %iota_add_fusion.3, s32[64]{0:T(128)S(1)} %get-tuple-element.6, s32[64]{0:T(128)S(1)} %get-tuple-element.5), kind=kOutput, calls=%fused_computation.23 | convolution fusion | flops 1615331328 | bytes 9185792 | tf_op jit(solution)/shard_map/dot_general | solution.py:40
  35.9 7.9 %fusion.17 = bf16[64,1024]{1,0:T(8,128)(2,1)S(1)} fusion(f32[64,1024]{1,0:T(8,128)S(1)} %fusion.16, f32[2048,1024]{0,1:T(8,128)} %collective-permute-done, s32[2048]{0:T(1024)S(1)} %iota_add_fusion, s32[64]{0:T(128)S(1)} %get-tuple-element.6, s32[64]{0:T(128)S(1)} %get-tuple-element.5), kind=kOutput, calls=%fused_computation.24 | convolution fusion | flops 1611202560 | bytes 8790528 | tf_op jit(solution)/shard_map/dot_general | solution.py:47
  43.8 1.2 gather_fusion.1
  45.0 0.9 broadcast_select_fusion.1
  45.9 78.5 %all-to-all-start = ((bf16[16,16,1024]{2,1,0:T(8,128)(2,1)}), bf16[16,16,1024]{2,1,0:T(8,128)(2,1)S(1)}, u32[]{:S(2)}, u32[]{:S(2)}) async-start(bf16[16,16,1024]{2,1,0:T(8,128)(2,1)} %broadcast_select_fusion.1), calls=%async_computation | async-start | bytes 1048576 | tf_op jit(solution)/shard_map/all_to_all | solution.py:62
  124.6 0.3 reshape.372
  125.0 1.7 %gather_fusion = s32[256]{0:T(256)S(1)} fusion(s32[4096]{0:T(1024)S(1)} %reshape.372, s32[1024]{0:T(1024)S(1)} %pad_clamp_fusion.1), kind=kCustom, calls=%fused_computation | custom fusion | bytes 3072 | tf_op jit(solution)/shard_map/gather | solution.py:68
  127.0 0.6 convert_reduce_fusion
  127.5 11.1 %all-to-all-done = bf16[16,16,1024]{2,1,0:T(8,128)(2,1)S(1)} async-done(((bf16[16,16,1024]{2,1,0:T(8,128)(2,1)}), bf16[16,16,1024]{2,1,0:T(8,128)(2,1)S(1)}, u32[]{:S(2)}, u32[]{:S(2)}) %all-to-all-start) | async-done | bytes 524320 | tf_op jit(solution)/shard_map/all_to_all | solution.py:62
  138.7 1.3 convolution_divide_fusion
  (30 shorter events, 0.9 us)
Async XLA Ops:
  6.9 5.7 %copy-start = (f32[1024,2048]{1,0:T(8,128)}, f32[1024,2048]{1,0:T(8,128)S(1)}, u32[]{:S(2)}) copy-start(f32[1024,2048]{1,0:T(8,128)S(1)} %fusion.22) | copy-start | bytes 25165828
  6.9 8.6 %copy-start.2 = (s32[64,2]{0,1:T(2,128)S(1)}, s32[64,2]{0,1:T(2,128)}, u32[]{:S(2)}) copy-start(s32[64,2]{0,1:T(2,128)} %param.10) | copy-start | bytes 1540
  12.6 23.3 %collective-permute-start = (f32[2048,1024]{0,1:T(8,128)}, f32[2048,1024]{0,1:T(8,128)}, u32[]{:S(2)}, u32[]{:S(2)}) collective-permute-start(f32[2048,1024]{0,1:T(8,128)} %fusion.6), channel_id=1, source_target_pairs={{1,0},{2,1},{3,2},{4,3},{5,4},{6,5},{7,6},{8,7},{9,8},{10,9},{11,1... | collective-permute-start | bytes 25165832 | tf_op jit(solution)/shard_map/ppermute | solution.py:12
  20.7 10.0 %slice-start = ((s8[8388608]{0:T(1024)(128)(4,1)}), s8[4194304]{0:T(1024)(128)(4,1)S(1)}, s32[]{:S(2)}) async-start(s8[8388608]{0:T(1024)(128)(4,1)} %bitcast.35), calls=%async_computation.1 | async-start | bytes 8388608
  25.7 5.0 %slice-start.1 = ((s8[8388608]{0:T(1024)(128)(4,1)}), s8[4194304]{0:T(1024)(128)(4,1)S(1)}, s32[]{:S(2)}) async-start(s8[8388608]{0:T(1024)(128)(4,1)} %bitcast.35), calls=%async_computation.2 | async-start | bytes 8388608
  35.9 88.5 %copy-start.1 = (s32[1024,4]{0,1:T(4,128)S(1)}, s32[1024,4]{0,1:T(4,128)}, u32[]{:S(2)}) copy-start(s32[1024,4]{0,1:T(4,128)} %param.11) | copy-start | bytes 49156
  45.9 92.8 %all-to-all-start = ((bf16[16,16,1024]{2,1,0:T(8,128)(2,1)}), bf16[16,16,1024]{2,1,0:T(8,128)(2,1)S(1)}, u32[]{:S(2)}, u32[]{:S(2)}) async-start(bf16[16,16,1024]{2,1,0:T(8,128)(2,1)} %broadcast_select_fusion.1), calls=%async_computation | async-start | bytes 1048576 | tf_op jit(solution)/shard_map/all_to_all | solution.py:62
where the time goes:
time: 140 us
  starting transfers between devices  80 us (57%)
  matrix products  31.9 us (23%)
  waiting for transfers between devices  11.1 us (8%)
  other arithmetic  10.6 us (8%)
  local copies, waits for them, and re-layouts  6.12 us (4%)
    all_to_all x1, starting transfers between devices, local(): lax.all_to_all(packed, 'genome', split_axis=0, concat_axis=0, tiled=True)  78.5 us
    dot_general x3, matrix products, local(): jnp.dot(covered(positions, gene_span), squares, precision=lax.Precision.H...  15.1 us
    all_to_all x1, waiting for transfers between devices, local(): lax.all_to_all(packed, 'genome', split_axis=0, concat_axis=0, tiled=True)  11.1 us
    dot_general x1, matrix products, local(): jnp.dot(covered(beyond, gene_span), following, precision=lax.Precision.HI...  7.89 us
    dot_general x3, matrix products, local(): jnp.dot(factor[block], trimmed[block], preferred_element_type=jnp.float32)  7.61 us
    select_n x1, other arithmetic, local(): squares = jnp.where(usable[:, None], coloured * coloured, 0.0)  4.67 us
  transfers between devices with their start and end apart: 2, of which 1 were waited for; matrix products, arithmetic and copies ran while one was open for 18% of the time, Pallas kernels for 0%

commit v1 on v0

v1 whole, which is shorter than its diff:
```python
import functools

import jax
import jax.numpy as jnp
from jax import lax
from jax.experimental import pallas as pl
from jax.experimental.pallas import tpu as pltpu
from jax.sharding import PartitionSpec as P

PATHWAYS = 4096
QUAD = 4
CHUNK = 512
COLS = 256
VMEM = pltpu.MemorySpace.VMEM
SMEM = pltpu.MemorySpace.SMEM


def to_column(row, classes):
    genes = row.shape[1]
    each = genes // classes
    at = lax.broadcasted_iota(jnp.int32, (genes, genes), 0)
    lane = lax.broadcasted_iota(jnp.int32, (genes, genes), 1)
    hit = lane == (at % each) * classes + at // each
    values = jnp.where(hit, row.astype(jnp.float32), 0.0)
    return jnp.sum(values, axis=1, keepdims=True).astype(jnp.int32)


def block_kernel(classes, sets, info, *refs):
    spans, (factor, normals) = refs[:sets], refs[sets:sets + 2]
    outs = refs[sets + 2:2 * sets + 2]
    vectors, lower, upper = refs[2 * sets + 2:]
    genes = spans[0].shape[1]
    step = pl.program_id(0)
    base, length, rank = info[0], info[1], info[2]

    @pl.when(step == 0)
    def _():
        row = lax.broadcasted_iota(jnp.int32, normals.shape[1:], 0)
        vectors[...] = jnp.where(row < rank, normals[0].astype(jnp.float32), 0.0).astype(jnp.bfloat16)
        for at in range(sets):
            span = spans[at][...]
            rows = pl.ds(at * genes, genes)
            lower[rows, :] = to_column(span[0:1], classes) - base
            upper[rows, :] = jnp.minimum(to_column(span[1:2], classes) - base, length)
            outs[at][...] = jnp.zeros(outs[at].shape, jnp.float32)

    @pl.when(step * CHUNK < length)
    def _():
        slot = step * CHUNK + lax.broadcasted_iota(jnp.int32, (sets * genes, CHUNK), 1)
        mask = (slot >= lower[...]) & (slot < upper[...])
        mask = jnp.where(mask, 1.0, 0.0).astype(jnp.bfloat16)
        sims = vectors.shape[1]
        for col in range(0, sims, COLS):
            cols = slice(col, col + COLS)
            coloured = jnp.dot(factor[0], vectors[:, cols], preferred_element_type=jnp.float32)
            square = coloured * coloured
            high = square.astype(jnp.bfloat16)
            low = (square - high.astype(jnp.float32)).astype(jnp.bfloat16)
            total = jnp.dot(mask, high, preferred_element_type=jnp.float32)
            total = total + jnp.dot(mask, low, preferred_element_type=jnp.float32)
            for at in range(sets):
                outs[at][:, cols] += total[at * genes:(at + 1) * genes]


def block_sums(block, classes, info, spans, factor, normals):
    sets = len(spans)
    genes = spans[0].shape[1]
    _, capacity, rank_cap = factor.shape
    sims = normals.shape[2]
    whole = pl.BlockSpec((genes, sims), lambda i, info: (0, 0))
    last = lambda i, info: (block, jnp.minimum(i, (info[1] - 1) // CHUNK), 0)
    return pl.pallas_call(
        functools.partial(block_kernel, classes, sets),
        out_shape=[jax.ShapeDtypeStruct((genes, sims), jnp.float32)] * sets,
        grid_spec=pltpu.PrefetchScalarGridSpec(
            num_scalar_prefetch=1,
            grid=(capacity // CHUNK,),
            in_specs=[pl.BlockSpec((2, genes), lambda i, info: (0, 0))] * sets
            + [
                pl.BlockSpec((1, CHUNK, rank_cap), last),
                pl.BlockSpec((1, rank_cap, sims), lambda i, info: (block, 0, 0)),
            ],
            out_specs=[whole] * sets,
            scratch_shapes=[
                pltpu.VMEM((rank_cap, sims), jnp.bfloat16),
                pltpu.VMEM((sets * genes, 1), jnp.int32),
                pltpu.VMEM((sets * genes, 1), jnp.int32),
            ],
        ),
        cost_estimate=pl.CostEstimate(
            flops=6 * capacity * rank_cap * sims, bytes_accessed=4 << 20, transcendentals=0
        ),
        name=f"block{block}",
    )(info, *spans, factor, normals)


def combine_kernel(classes, capacity, where, first, second, third, back, *refs):
    outs, stat = refs[:-1], refs[-1]
    each = outs[0].shape[0]
    total = first[...] + second[...] + third[...] + back[...]
    total = total / capacity
    for at in range(classes):
        stat[at] = total[at * each:(at + 1) * each]
    for ahead in range(classes):
        outs[ahead][...] = stat[lax.rem(where[0] + ahead, classes)].astype(jnp.bfloat16)


def combine(classes, capacity, where, parts):
    genes, sims = parts[0].shape
    piece = jax.ShapeDtypeStruct((genes // classes, sims), jnp.bfloat16)
    return pl.pallas_call(
        functools.partial(combine_kernel, classes, capacity),
        out_shape=[piece] * classes,
        in_specs=[pl.BlockSpec(memory_space=SMEM)] + [pl.BlockSpec(memory_space=VMEM)] * 4,
        out_specs=[pl.BlockSpec(memory_space=VMEM)] * classes,
        scratch_shapes=[pltpu.VMEM((classes, genes // classes, sims), jnp.float32)],
        name="combine",
    )(where, *parts)


def member_kernel(classes, flips, genes_dev, where, paths, member, count):
    plane, inner = where[0], where[1]
    rows, pairs = member.shape
    genes = paths.shape[1]
    each = genes_dev // classes
    device = plane * QUAD + inner
    own = paths[pl.ds(inner, 1), :] - device * rows
    own = jnp.where((own >= 0) & (own < rows), own, 0).astype(jnp.float32)
    own = jnp.broadcast_to(own, (8, genes)).astype(jnp.bfloat16)
    col = lax.broadcasted_iota(jnp.int32, (genes, pairs), 1)
    gene = lax.broadcasted_iota(jnp.int32, (genes, pairs), 0)
    part = col // genes_dev
    source_in = jnp.zeros(col.shape, jnp.int32)
    for at, flip in enumerate(flips):
        source_in = jnp.where(part == at, inner ^ flip, source_in)
    behind = (col % genes_dev) // each
    source_plane = plane - behind
    source_plane = jnp.where(source_plane < 0, source_plane + classes, source_plane)
    source = source_plane * QUAD + source_in
    named = source * genes_dev + (col % each) * classes + plane
    pick = jnp.where(gene == named, 1.0, 0.0).astype(jnp.bfloat16)
    ids = jnp.dot(own, pick, preferred_element_type=jnp.float32)[0:1]
    row = lax.broadcasted_iota(jnp.int32, (rows, pairs), 0).astype(jnp.float32)
    found = jnp.where(row == ids, 1.0, 0.0)
    member[...] = found.astype(jnp.bfloat16)
    count[...] = jnp.sum(found, axis=1, keepdims=True)


def members(classes, flips, genes_dev, rows, where, paths):
    pairs = QUAD * genes_dev
    return pl.pallas_call(
        functools.partial(member_kernel, classes, flips, genes_dev),
        out_shape=[
            jax.ShapeDtypeStruct((rows, pairs), jnp.bfloat16),
            jax.ShapeDtypeStruct((rows, 1), jnp.float32),
        ],
        in_specs=[pl.BlockSpec(memory_space=SMEM), pl.BlockSpec(memory_space=VMEM)],
        out_specs=[pl.BlockSpec(memory_space=VMEM)] * 2,
        name="members",
    )(where, paths)


def score_kernel(member, count, first, second, third, fourth, out):
    genes = first.shape[0]
    total = jnp.zeros(out.shape, jnp.float32)
    for at, part in enumerate((first, second, third, fourth)):
        total = total + jnp.dot(
            member[:, at * genes:(at + 1) * genes], part[...], preferred_element_type=jnp.float32
        )
    out[...] = total / count[...]


def score(member, count, parts):
    rows = member.shape[0]
    return pl.pallas_call(
        score_kernel,
        out_shape=jax.ShapeDtypeStruct((rows, parts[0].shape[1]), jnp.float32),
        in_specs=[pl.BlockSpec(memory_space=VMEM)] * 6,
        out_specs=pl.BlockSpec(memory_space=VMEM),
        name="score",
    )(member, count, *parts)


def local(factor, normals, block_len, block_rank, gene_span, gene_pathways):
    block_count, capacity, _ = factor.shape
    genes = gene_span.shape[0]
    device = lax.axis_index("genome")
    size = lax.axis_size("genome")
    classes = size // QUAD
    each = genes // classes
    plane, inner = device // QUAD, device % QUAD
    send = functools.partial(lax.ppermute, axis_name="genome")

    own = gene_span.T
    before = send(own, perm=[(i, i + 1) for i in range(size - 1)])

    def info(block):
        base = (device * block_count + block) * capacity
        return jnp.stack([base, block_len[block], block_rank[block]])

    sums = functools.partial(block_sums, factor=factor, normals=normals)
    (first,) = sums(1, classes, info(1), [own])
    second, lent = sums(0, classes, info(0), [own, before])
    back = send(lent, perm=[(i + 1, i) for i in range(size - 1)])
    (third,) = sums(2, classes, info(2), [own])
    where = jnp.stack([plane, inner])
    pieces = combine(classes, float(capacity), where, [first, second, third, back])

    arrived = [pieces[0]]
    for ahead in range(1, classes):
        route = [
            (c * QUAD + j, (c + ahead) % classes * QUAD + j)
            for c in range(classes)
            for j in range(QUAD)
        ]
        arrived.append(send(pieces[ahead], perm=route))
    mine = jnp.concatenate(arrived, axis=0)
    flip = lambda x, bit: send(x, perm=[(i, i ^ bit) for i in range(size)])
    across = flip(mine, 2)
    partner = flip(mine, 1)
    corner = flip(across, 1)

    rows = PATHWAYS // size
    member, count = members(classes, (0, 2, 1, 3), genes, rows, where, gene_pathways.T)
    return score(member, count, [mine, across, partner, corner])


def solution(mesh):
    in_specs = (
        P(("groups", "genome"), None, None),
        P(("groups", "genome"), None, None),
        P(("groups", "genome")),
        P(("groups", "genome")),
        P(("groups", "genome"), None),
        P("groups", None),
    )
    out_specs = P(("groups", "genome"), None)
    return jax.shard_map(local, mesh=mesh, in_specs=in_specs, out_specs=out_specs, check_vma=False)
```

time: 140 us -> 56.2 us (0.40)
  starting transfers between devices: 80 us -> 15.4 us
  matrix products: 31.9 us -> 0 us
  Pallas kernels: 0 us -> 22.9 us
  other arithmetic: 10.6 us -> 5.55 us
  waiting for transfers between devices: 11.1 us -> 6.07 us
    all_to_all x1 -> x0, starting transfers between devices: 78.5 us -> none  [local(): lax.all_to_all(packed, 'genome', split_axis=0, concat_axis=0, tiled=True)]
    dot_general x8 -> x0, matrix products: 31.9 us -> none  [the longest x3 15.1 us: local(): jnp.dot(covered(positions, gene_span), squares, precision=lax.Precision.H...]
    pallas_call x0 -> x6, Pallas kernels: none -> 22.9 us  [the longest x3 16.3 us: block_sums(): pl.pallas_call(functools.partial(block_kernel, classes, sets), out_shape=...]
    ppermute x1 -> x8, starting transfers between devices: 1.46 us -> 15.4 us  [the longest x3 11.1 us: local(): arrived.append(send(pieces[ahead], perm=route))]
    all_to_all x1 -> x0, waiting for transfers between devices: 11.1 us -> none  [local(): lax.all_to_all(packed, 'genome', split_axis=0, concat_axis=0, tiled=True)]
    select_n x7 -> x0, other arithmetic: 7.35 us -> none  [the longest x1 4.67 us: local(): squares = jnp.where(usable[:, None], coloured * coloured, 0.0)]
    ppermute x1 -> x8, waiting for transfers between devices: 0.01 us -> 6.07 us  [the longest x3 4.34 us: local(): flip = lambda x, bit: send(x, perm=[(i, i ^ bit) for i in range(size)])]
    another operation x0 -> x3, other arithmetic: none -> 5.55 us  [the longest x2 4.97 us: info(): return jnp.stack([base, block_len[block], block_rank[block]])]
  transfers between devices with their start and end apart: 2 -> 8, of which waited for: 1 -> 3; matrix products, arithmetic and copies ran while one was open for 18% -> 16% of each run, Pallas kernels for 0% -> 20%
where the time goes in v1:
time: 56.2 us; the launch traced here: 55.6 us
  Pallas kernels  22.9 us (41%)
  starting transfers between devices  15.4 us (27%)
  waiting for transfers between devices  6.07 us (11%)
  local copies, waits for them, and re-layouts  5.55 us (10%)
  other arithmetic  5.55 us (10%)
    pallas_call x3, Pallas kernels, block_sums(): pl.pallas_call(functools.partial(block_kernel, classes, sets), out_shape=...  16.3 us
    ppermute x3, starting transfers between devices, local(): arrived.append(send(pieces[ahead], perm=route))  11.1 us
    another operation x2, other arithmetic, info(): return jnp.stack([base, block_len[block], block_rank[block]])  4.97 us
    ppermute x3, waiting for transfers between devices, local(): flip = lambda x, bit: send(x, perm=[(i, i ^ bit) for i in range(size)])  4.34 us
    pallas_call x1, Pallas kernels, score(): pl.pallas_call(score_kernel, out_shape=jax.ShapeDtypeStruct((rows, parts[...  2.91 us
    slice x2, local copies, waits for them, and re-layouts, info(): return jnp.stack([base, block_len[block], block_rank[block]])  2.84 us
    unnamed x15, local copies, waits for them, and re-layouts  2.71 us
    ppermute x1, starting transfers between devices, local(): before = send(own, perm=[(i, i + 1) for i in range(size - 1)])  2.39 us
  transfers between devices with their start and end apart: 8, of which 3 were waited for; matrix products, arithmetic and copies ran while one was open for 16% of the time, Pallas kernels for 20%

profile of v1, /device:TPU:0, one launch (start us, length us, event | category | flops | bytes accessed | tf_op | source)
XLA Modules:
  0.0 55.6 jit_solution(1391364579881471607)
XLA Ops:
  0.0 2.4 %collective-permute-start = (s32[2,64]{1,0:T(2,128)}, s32[2,64]{1,0:T(2,128)S(1)}, u32[]{:S(2)}, u32[]{:S(2)}) collective-permute-start(s32[2,64]{1,0:T(2,128)} %bitcast.8), channel_id=1, source_target_pairs={{0,1},{1,2},{2,3},{3,4},{4,5},{5,6},{6,7},{7,8},{8,9},{9,10},{10,1... | collective-permute-start | bytes 1544 | tf_op jit(solution)/shard_map/ppermute | solution.py:195
  2.4 1.4 %fusion = (s32[1]{0:T(128)}, s32[1]{0:T(128)}, s32[1]{0:T(128)}) fusion(s32[3]{0:T(128)} %param.8), kind=kLoop, calls=%fused_computation.8 | loop fusion | bytes 24 | tf_op jit(solution)/shard_map/slice | solution.py:199
  3.8 1.4 %fusion.1 = (s32[1]{0:T(128)}, s32[1]{0:T(128)}, s32[1]{0:T(128)}) fusion(s32[3]{0:T(128)} %param.9), kind=kLoop, calls=%fused_computation.9 | loop fusion | bytes 24 | tf_op jit(solution)/shard_map/slice | solution.py:199
  5.3 0.6 %pad_add_fusion.where = s32[2]{0:T(128)} fusion(s32[1]{0:T(128)} %bitcast.1, s32[1]{0:T(128)} %bitcast), kind=kLoop, calls=%fused_computation.4 | loop fusion | flops 2 | bytes 16 | tf_op jit(solution)/shard_map/stack | solution.py:206
  5.8 3.1 %pad_add_fusion.1 = (s32[3]{0:T(128)}, s32[3]{0:T(128)}) fusion(s32[1]{0:T(128)} %get-tuple-element.25, s32[1]{0:T(128)} %get-tuple-element.22, s32[1]{0:T(128)} %bitcast.3, s32[1]{0:T(128)} %get-tuple-element.24, s32[1]{0:T(128)} %get-tuple-element.21, s32[1]{0:T(128)} %bitcast.6), kind=kLoop, calls=%fused_computation.5 | loop fusion | flops 12 | bytes 48 | tf_op jit(solution)/shard_map/stack | solution.py:199
  8.9 4.8 %block1.1.first = f32[64,1024]{1,0:T(8,128)} custom-call(s32[3]{0:T(128)} %get-tuple-element.27.info, s32[2,64]{1,0:T(2,128)} %bitcast.9, bf16[3,2048,256]{2,1,0:T(8,128)(2,1)} %refs_1_.3, bf16[3,256,1024]{2,1,0:T(8,128)(2,1)} %refs_2_.5), custom_call_target="tpu_custom_call" | custom-call | flops 3221225472 | bytes 4194304 | tf_op jit(solution)/shard_map/block1/pallas_call | solution.py:72
  13.8 1.9 %pad_add_fusion.2.info = s32[3]{0:T(128)} fusion(s32[1]{0:T(128)} %get-tuple-element.26, s32[1]{0:T(128)} %get-tuple-element.23, s32[1]{0:T(128)} %bitcast.5), kind=kLoop, calls=%fused_computation.6 | loop fusion | flops 6 | bytes 24 | tf_op jit(solution)/shard_map/stack | solution.py:199
  15.6 0.6 %copy-done.5 = s32[2,64]{1,0:T(2,128)} copy-done((s32[2,64]{1,0:T(2,128)}, s32[2,64]{1,0:T(2,128)S(1)}, u32[]{:S(2)}) %copy-start.5) | copy-done | bytes 536
  16.2 6.7 %block0.1 = (f32[64,1024]{1,0:T(8,128)}, f32[64,1024]{1,0:T(8,128)}) custom-call(s32[3]{0:T(128)} %pad_add_fusion.2.info, s32[2,64]{1,0:T(2,128)} %bitcast.10, s32[2,64]{1,0:T(2,128)} %copy-done.5, bf16[3,2048,256]{2,1,0:T(8,128)(2,1)} %refs_1_.3, bf16[3,256,1024]{2,1,0:T(8,128)(2,1)} %refs_2_.5), custom_call_target="tpu_custom_call" | custom-call | flops 3221225472 | bytes 4194304 | tf_op jit(solution)/shard_map/block0/pallas_call | solution.py:72
  22.9 1.3 %collective-permute-start.1 = (f32[64,1024]{1,0:T(8,128)}, f32[64,1024]{1,0:T(8,128)S(1)}, u32[]{:S(2)}, u32[]{:S(2)}) collective-permute-start(f32[64,1024]{1,0:T(8,128)} %get-tuple-element.16), channel_id=1, source_target_pairs={{1,0},{2,1},{3,2},{4,3},{5,4},{6,5},{7,6},{8,7},{9,8},{10,9},{11,1... | collective-permute-start | bytes 786440 | tf_op jit(solution)/shard_map/ppermute | solution.py:204
  24.2 4.8 %block2.1.third = f32[64,1024]{1,0:T(8,128)} custom-call(s32[3]{0:T(128)} %get-tuple-element.28.info, s32[2,64]{1,0:T(2,128)} %bitcast.11, bf16[3,2048,256]{2,1,0:T(8,128)(2,1)} %refs_1_.3, bf16[3,256,1024]{2,1,0:T(8,128)(2,1)} %refs_2_.5), custom_call_target="tpu_custom_call" | custom-call | flops 3221225472 | bytes 4194304 | tf_op jit(solution)/shard_map/block2/pallas_call | solution.py:72
  29.0 0.6 %collective-permute-done.1.back = f32[64,1024]{1,0:T(8,128)S(1)} collective-permute-done((f32[64,1024]{1,0:T(8,128)}, f32[64,1024]{1,0:T(8,128)S(1)}, u32[]{:S(2)}, u32[]{:S(2)}) %collective-permute-start.1) | collective-permute-done | bytes 262176 | tf_op jit(solution)/shard_map/ppermute | solution.py:204
  29.6 0.7 %copy-done = f32[64,1024]{1,0:T(8,128)} copy-done((f32[64,1024]{1,0:T(8,128)}, f32[64,1024]{1,0:T(8,128)S(1)}, u32[]{:S(2)}) %copy-start) | copy-done | bytes 262168
  30.3 1.9 %combine.1 = (bf16[16,1024]{1,0:T(8,128)(2,1)}, bf16[16,1024]{1,0:T(8,128)(2,1)}, bf16[16,1024]{1,0:T(8,128)(2,1)}, bf16[16,1024]{1,0:T(8,128)(2,1)}) custom-call(s32[2]{0:T(128)} %pad_add_fusion.where, f32[64,1024]{1,0:T(8,128)} %block1.1.first, f32[64,1024]{1,0:T(8,128)} %get-tuple-element.15.second, f32[64,1024]{1,0:T(8,128)} %block2.1.third, ...), custom_call_target="tpu_custom_call" | custom-call | tf_op jit(solution)/shard_map/combine/pallas_call | solution.py:111
  32.3 6.2 %collective-permute-start.2 = (bf16[16,1024]{1,0:T(8,128)(2,1)}, bf16[16,1024]{1,0:T(8,128)(2,1)S(1)}, u32[]{:S(2)}, u32[]{:S(2)}) collective-permute-start(bf16[16,1024]{1,0:T(8,128)(2,1)} %get-tuple-element.18), channel_id=1, source_target_pairs={{0,4},{1,5},{2,6},{3,7},{4,8},{5,9},{6,10},{7,11},{8,12},{9,13},{1... | collective-permute-start | bytes 98312 | tf_op jit(solution)/shard_map/ppermute | solution.py:216
  38.5 2.0 %collective-permute-start.3 = (bf16[16,1024]{1,0:T(8,128)(2,1)}, bf16[16,1024]{1,0:T(8,128)(2,1)S(1)}, u32[]{:S(2)}, u32[]{:S(2)}) collective-permute-start(bf16[16,1024]{1,0:T(8,128)(2,1)} %get-tuple-element.19), channel_id=1, source_target_pairs={{0,8},{1,9},{2,10},{3,11},{4,12},{5,13},{6,14},{7,15},{8,0},{9,1},... | collective-permute-start | bytes 98312 | tf_op jit(solution)/shard_map/ppermute | solution.py:216
  40.5 2.9 %collective-permute-start.4 = (bf16[16,1024]{1,0:T(8,128)(2,1)}, bf16[16,1024]{1,0:T(8,128)(2,1)S(1)}, u32[]{:S(2)}, u32[]{:S(2)}) collective-permute-start(bf16[16,1024]{1,0:T(8,128)(2,1)} %get-tuple-element.20), channel_id=1, source_target_pairs={{0,12},{1,13},{2,14},{3,15},{4,0},{5,1},{6,2},{7,3},{8,4},{9,5},{1... | collective-permute-start | bytes 98312 | tf_op jit(solution)/shard_map/ppermute | solution.py:216
  43.4 0.8 %constant_dynamic-update-slice_fusion.3 = bf16[64,1024]{1,0:T(8,128)(2,1)S(1)} fusion(bf16[16,1024]{1,0:T(8,128)(2,1)} %get-tuple-element.17), kind=kLoop, calls=%fused_computation.3 | loop fusion | bytes 65536
  44.1 1.1 %collective-permute-done.4 = bf16[16,1024]{1,0:T(8,128)(2,1)S(1)} collective-permute-done((bf16[16,1024]{1,0:T(8,128)(2,1)}, bf16[16,1024]{1,0:T(8,128)(2,1)S(1)}, u32[]{:S(2)}, u32[]{:S(2)}) %collective-permute-start.4) | collective-permute-done | bytes 32800 | tf_op jit(solution)/shard_map/ppermute | solution.py:216
  45.3 0.6 %collective-permute-start.5 = (bf16[64,1024]{1,0:T(8,128)(2,1)S(1)}, bf16[64,1024]{1,0:T(8,128)(2,1)S(1)}, u32[]{:S(2)}, u32[]{:S(2)}) collective-permute-start(bf16[64,1024]{1,0:T(8,128)(2,1)S(1)} %constant_dynamic-update-slice_fusion.first), channel_id=1, source_target_pairs={{0,2},{1,3},{2,0},{3,1},{4,6},{5,7},{6,4},{7,5},{8,10},{9,11},{10,... | collective-permute-start | bytes 393224 | tf_op jit(solution)/shard_map/ppermute | solution.py:218
  45.9 4.3 %collective-permute-done.5.second = bf16[64,1024]{1,0:T(8,128)(2,1)S(1)} collective-permute-done((bf16[64,1024]{1,0:T(8,128)(2,1)S(1)}, bf16[64,1024]{1,0:T(8,128)(2,1)S(1)}, u32[]{:S(2)}, u32[]{:S(2)}) %collective-permute-start.5) | collective-permute-done | bytes 131104 | tf_op jit(solution)/shard_map/ppermute | solution.py:218
  50.2 1.7 %members.1 = (bf16[256,256]{1,0:T(8,128)(2,1)}, f32[256,1]{1,0:T(8,128)}) custom-call(s32[2]{0:T(128)} %pad_add_fusion.where, s32[4,1024]{1,0:T(4,128)} %bitcast.7), custom_call_target="tpu_custom_call" | custom-call | tf_op jit(solution)/shard_map/members/pallas_call | solution.py:151
  52.0 0.6 %copy-done.3 = bf16[64,1024]{1,0:T(8,128)(2,1)} copy-done((bf16[64,1024]{1,0:T(8,128)(2,1)}, bf16[64,1024]{1,0:T(8,128)(2,1)S(1)}, u32[]{:S(2)}) %copy-start.3) | copy-done | bytes 131096
  52.7 2.9 %score.1 = f32[256,1024]{1,0:T(8,128)} custom-call(bf16[256,256]{1,0:T(8,128)(2,1)} %get-tuple-element.13.member, f32[256,1]{1,0:T(8,128)} %get-tuple-element.14.count, bf16[64,1024]{1,0:T(8,128)(2,1)} %copy-done.1, bf16[64,1024]{1,0:T(8,128)(2,1)} %copy-done.2, bf16[64,1024]{1,0:T(8,128)(2,1)} %copy-done.3, bf16[64,1024]{1,0:T(8,128)(2,1)} %copy-done.4), custom_call_target="tpu_custom_call" | custom-call | tf_op jit(solution)/shard_map/score/pallas_call | solution.py:175
  (19 shorter events, 0.1 us)
Async XLA Ops:
  0.0 15.6 %collective-permute-start = (s32[2,64]{1,0:T(2,128)}, s32[2,64]{1,0:T(2,128)S(1)}, u32[]{:S(2)}, u32[]{:S(2)}) collective-permute-start(s32[2,64]{1,0:T(2,128)} %bitcast.8), channel_id=1, source_target_pairs={{0,1},{1,2},{2,3},{3,4},{4,5},{5,6},{6,7},{7,8},{8,9},{9,10},{10,1... | collective-permute-start | bytes 1544 | tf_op jit(solution)/shard_map/ppermute | solution.py:195
  15.6 0.6 %copy-start.5 = (s32[2,64]{1,0:T(2,128)}, s32[2,64]{1,0:T(2,128)S(1)}, u32[]{:S(2)}) copy-start(s32[2,64]{1,0:T(2,128)S(1)} %collective-permute-done.refs_1_) | copy-start | bytes 1540
  22.9 6.7 %collective-permute-start.1 = (f32[64,1024]{1,0:T(8,128)}, f32[64,1024]{1,0:T(8,128)S(1)}, u32[]{:S(2)}, u32[]{:S(2)}) collective-permute-start(f32[64,1024]{1,0:T(8,128)} %get-tuple-element.16), channel_id=1, source_target_pairs={{1,0},{2,1},{3,2},{4,3},{5,4},{6,5},{7,6},{8,7},{9,8},{10,9},{11,1... | collective-permute-start | bytes 786440 | tf_op jit(solution)/shard_map/ppermute | solution.py:204
  29.6 0.7 %copy-start = (f32[64,1024]{1,0:T(8,128)}, f32[64,1024]{1,0:T(8,128)S(1)}, u32[]{:S(2)}) copy-start(f32[64,1024]{1,0:T(8,128)S(1)} %collective-permute-done.1.back) | copy-start | bytes 786436
  32.3 11.9 %collective-permute-start.2 = (bf16[16,1024]{1,0:T(8,128)(2,1)}, bf16[16,1024]{1,0:T(8,128)(2,1)S(1)}, u32[]{:S(2)}, u32[]{:S(2)}) collective-permute-start(bf16[16,1024]{1,0:T(8,128)(2,1)} %get-tuple-element.18), channel_id=1, source_target_pairs={{0,4},{1,5},{2,6},{3,7},{4,8},{5,9},{6,10},{7,11},{8,12},{9,13},{1... | collective-permute-start | bytes 98312 | tf_op jit(solution)/shard_map/ppermute | solution.py:216
  38.5 5.7 %collective-permute-start.3 = (bf16[16,1024]{1,0:T(8,128)(2,1)}, bf16[16,1024]{1,0:T(8,128)(2,1)S(1)}, u32[]{:S(2)}, u32[]{:S(2)}) collective-permute-start(bf16[16,1024]{1,0:T(8,128)(2,1)} %get-tuple-element.19), channel_id=1, source_target_pairs={{0,8},{1,9},{2,10},{3,11},{4,12},{5,13},{6,14},{7,15},{8,0},{9,1},... | collective-permute-start | bytes 98312 | tf_op jit(solution)/shard_map/ppermute | solution.py:216
  40.5 4.8 %collective-permute-start.4 = (bf16[16,1024]{1,0:T(8,128)(2,1)}, bf16[16,1024]{1,0:T(8,128)(2,1)S(1)}, u32[]{:S(2)}, u32[]{:S(2)}) collective-permute-start(bf16[16,1024]{1,0:T(8,128)(2,1)} %get-tuple-element.20), channel_id=1, source_target_pairs={{0,12},{1,13},{2,14},{3,15},{4,0},{5,1},{6,2},{7,3},{8,4},{9,5},{1... | collective-permute-start | bytes 98312 | tf_op jit(solution)/shard_map/ppermute | solution.py:216
  45.3 6.7 %copy-start.1 = (bf16[64,1024]{1,0:T(8,128)(2,1)}, bf16[64,1024]{1,0:T(8,128)(2,1)S(1)}, u32[]{:S(2)}) copy-start(bf16[64,1024]{1,0:T(8,128)(2,1)S(1)} %constant_dynamic-update-slice_fusion.first) | copy-start | bytes 393220
  45.3 5.0 %collective-permute-start.5 = (bf16[64,1024]{1,0:T(8,128)(2,1)S(1)}, bf16[64,1024]{1,0:T(8,128)(2,1)S(1)}, u32[]{:S(2)}, u32[]{:S(2)}) collective-permute-start(bf16[64,1024]{1,0:T(8,128)(2,1)S(1)} %constant_dynamic-update-slice_fusion.first), channel_id=1, source_target_pairs={{0,2},{1,3},{2,0},{3,1},{4,6},{5,7},{6,4},{7,5},{8,10},{9,11},{10,... | collective-permute-start | bytes 393224 | tf_op jit(solution)/shard_map/ppermute | solution.py:218
  45.9 6.1 %collective-permute-start.6 = (bf16[64,1024]{1,0:T(8,128)(2,1)S(1)}, bf16[64,1024]{1,0:T(8,128)(2,1)S(1)}, u32[]{:S(2)}, u32[]{:S(2)}) collective-permute-start(bf16[64,1024]{1,0:T(8,128)(2,1)S(1)} %constant_dynamic-update-slice_fusion.first), channel_id=1, source_target_pairs={{0,1},{1,0},{2,3},{3,2},{4,5},{5,4},{6,7},{7,6},{8,9},{9,8},{10,11... | collective-permute-start | bytes 393224 | tf_op jit(solution)/shard_map/ppermute | solution.py:218
  50.2 1.7 %copy-start.2 = (bf16[64,1024]{1,0:T(8,128)(2,1)}, bf16[64,1024]{1,0:T(8,128)(2,1)S(1)}, u32[]{:S(2)}) copy-start(bf16[64,1024]{1,0:T(8,128)(2,1)S(1)} %collective-permute-done.5.second) | copy-start | bytes 393220
  50.2 1.7 %collective-permute-start.7 = (bf16[64,1024]{1,0:T(8,128)(2,1)S(1)}, bf16[64,1024]{1,0:T(8,128)(2,1)S(1)}, u32[]{:S(2)}, u32[]{:S(2)}) collective-permute-start(bf16[64,1024]{1,0:T(8,128)(2,1)S(1)} %collective-permute-done.5.second), channel_id=1, source_target_pairs={{0,1},{1,0},{2,3},{3,2},{4,5},{5,4},{6,7},{7,6},{8,9},{9,8},{10,11... | collective-permute-start | bytes 393224 | tf_op jit(solution)/shard_map/ppermute | solution.py:218
  52.0 0.6 %copy-start.3 = (bf16[64,1024]{1,0:T(8,128)(2,1)}, bf16[64,1024]{1,0:T(8,128)(2,1)S(1)}, u32[]{:S(2)}) copy-start(bf16[64,1024]{1,0:T(8,128)(2,1)S(1)} %collective-permute-done.6.third) | copy-start | bytes 393220
  52.0 0.7 %copy-start.4 = (bf16[64,1024]{1,0:T(8,128)(2,1)}, bf16[64,1024]{1,0:T(8,128)(2,1)S(1)}, u32[]{:S(2)}) copy-start(bf16[64,1024]{1,0:T(8,128)(2,1)S(1)} %collective-permute-done.7.fourth) | copy-start | bytes 393220

commit v2 on v1

v2 whole, which is shorter than its diff:
```python
import functools

import jax
import jax.numpy as jnp
from jax import lax
from jax.experimental import pallas as pl
from jax.experimental.pallas import tpu as pltpu
from jax.sharding import PartitionSpec as P

PATHWAYS = 4096
QUAD = 4
CHUNK = 512
COLS = 256
LANES = 128
VMEM = pltpu.MemorySpace.VMEM
SMEM = pltpu.MemorySpace.SMEM


def gene_sums(prefix, parts, spans, out, base, length, classes):
    genes = spans.shape[1]
    each = genes // classes
    tiles = prefix.shape[0]

    @pl.loop(0, genes // 8)
    def _(group):
        for slot in range(8):
            spot = group * 8 + slot
            gene = (spot % each) * classes + spot // each
            lower = jnp.clip(spans[0, gene] - base, 0, length)
            upper = jnp.clip(spans[1, gene] - base, 0, length)
            for tile in range(tiles):
                parts[tile, slot * 8:slot * 8 + 8, :] = (
                    prefix[tile, pl.ds(upper, 8), :] - prefix[tile, pl.ds(lower, 8), :]
                )
        place = pl.ds(pl.multiple_of(group * 8, 8), 8)
        for tile in range(tiles):
            total = parts[tile, pl.ds(0, 8, stride=8), :]
            for sub in range(1, 8):
                total = total + parts[tile, pl.ds(sub, 8, stride=8), :]
            out[place, tile * LANES:(tile + 1) * LANES] = total


def running_sums(factor, normals, rank, length, vectors, prefix):
    rank_cap, sims = normals.shape
    tiles = sims // LANES
    row = lax.broadcasted_iota(jnp.int32, (rank_cap, LANES), 0)
    keep = jnp.where(row < rank, 1.0, 0.0).astype(jnp.bfloat16)
    for tile in range(tiles):
        cols = slice(tile * LANES, (tile + 1) * LANES)
        vectors[:, cols] = normals[:, cols] * keep
        prefix[tile, 0:8, :] = jnp.zeros((8, LANES), jnp.float32)

    @pl.loop(0, (length() + CHUNK - 1) // CHUNK)
    def _(chunk):
        start = pl.multiple_of(chunk * CHUNK, CHUNK)
        rows = factor[pl.ds(start, CHUNK), :]
        for col in range(0, sims, COLS):
            coloured = jnp.dot(rows, vectors[:, col:col + COLS], preferred_element_type=jnp.float32)
            square = coloured * coloured
            for part in range(COLS // LANES):
                tile = col // LANES + part
                run = prefix[tile, pl.ds(start, 8), :]
                for at in range(0, CHUNK, 8):
                    run = run + square[at:at + 8, part * LANES:(part + 1) * LANES]
                    prefix[tile, pl.ds(start + at + 8, 8), :] = run


def opening_kernel(classes, lens, ranks, spans, factor, normals, out, next_factor, next_normals, table,
                   lens_in, ranks_in, spans_in, factor_in, normals_in, vectors, prefix, parts, sems):
    block_count, capacity, _ = factor.shape
    copies = [
        pltpu.make_async_copy(source, target, sems.at[at])
        for at, (source, target) in enumerate([
            (ranks, ranks_in), (lens, lens_in), (normals.at[1], normals_in), (factor.at[1], factor_in),
            (spans, spans_in), (normals.at[0], next_normals.at[0]), (factor.at[0], next_factor.at[0]),
            (normals.at[2], next_normals.at[1]), (factor.at[2], next_factor.at[1]),
        ])
    ]
    for copy in copies:
        copy.start()
    for copy in copies[:4]:
        copy.wait()
    for block in range(block_count):
        table[block:block + 1, :] = jnp.full((1, LANES), ranks_in[block], jnp.int32)
        table[block_count + block:block_count + block + 1, :] = jnp.full((1, LANES), lens_in[block], jnp.int32)
    running_sums(factor_in, normals_in, ranks_in[1], lambda: lens_in[1], vectors, prefix)
    copies[4].wait()
    base = (lax.axis_index("genome") * block_count + 1) * capacity
    gene_sums(prefix, parts, spans_in, out, base, lens_in[1], classes)
    for copy in copies[5:]:
        copy.wait()


def block_kernel(block, at, block_count, classes, sets, table, *refs):
    spans, (factor, normals) = refs[:sets], refs[sets:sets + 2]
    outs = refs[sets + 2:2 * sets + 2]
    table_in, spans_in, vectors, prefix, parts, sems = refs[2 * sets + 2:]
    capacity = factor.shape[1]
    copies = [pltpu.make_async_copy(table, table_in, sems.at[0])]
    for own in range(sets):
        copies.append(pltpu.make_async_copy(spans[own], spans_in.at[own], sems.at[1 + own]))
    for copy in copies:
        copy.start()
    factor, normals = factor.at[at], normals.at[at]

    def length():
        for copy in copies:
            copy.wait()
        return table_in[block_count + block, 0]

    running_sums(factor, normals, table[block:block + 1, :], length, vectors, prefix)
    base = (lax.axis_index("genome") * block_count + block) * capacity
    for own in range(sets):
        gene_sums(prefix, parts, spans_in.at[own], outs[own], base, table_in[block_count + block, 0], classes)


def work_space(capacity, rank_cap, sims):
    return [
        pltpu.VMEM((rank_cap, sims), jnp.bfloat16),
        pltpu.VMEM((sims // LANES, capacity + 8, LANES), jnp.float32),
        pltpu.VMEM((sims // LANES, 64, LANES), jnp.float32),
    ]


ANY, IN_VMEM = pl.BlockSpec(memory_space=pl.ANY), pl.BlockSpec(memory_space=VMEM)
IN_HBM = pl.BlockSpec(memory_space=pltpu.MemorySpace.HBM)


def opening(classes, lens, ranks, spans, factor, normals):
    genes = spans.shape[1]
    block_count, capacity, rank_cap = factor.shape
    sims = normals.shape[2]
    shape = jax.ShapeDtypeStruct
    return pl.pallas_call(
        functools.partial(opening_kernel, classes),
        out_shape=[
            shape((genes, sims), jnp.float32),
            shape((block_count - 1, capacity, rank_cap), factor.dtype),
            shape((block_count - 1, rank_cap, sims), normals.dtype),
            shape((8, LANES), jnp.int32),
        ],
        in_specs=[IN_HBM] * 5,
        out_specs=[IN_VMEM] * 4,
        scratch_shapes=[
            pltpu.SMEM((block_count,), jnp.int32),
            pltpu.SMEM((block_count,), jnp.int32),
            pltpu.SMEM((2, genes), jnp.int32),
            pltpu.VMEM((capacity, rank_cap), factor.dtype),
            pltpu.VMEM((rank_cap, sims), normals.dtype),
        ] + work_space(capacity, rank_cap, sims) + [pltpu.SemaphoreType.DMA((9,))],
        compiler_params=pltpu.CompilerParams(vmem_limit_bytes=24 << 20),
        name="opening",
    )(lens, ranks, spans, factor, normals)


def block_sums(block, at, block_count, classes, table, spans, factor, normals):
    sets = len(spans)
    genes = spans[0].shape[1]
    _, capacity, rank_cap = factor.shape
    sims = normals.shape[2]
    return pl.pallas_call(
        functools.partial(block_kernel, block, at, block_count, classes, sets),
        out_shape=[jax.ShapeDtypeStruct((genes, sims), jnp.float32)] * sets,
        in_specs=[IN_VMEM] + [ANY] * sets + [IN_VMEM] * 2,
        out_specs=[IN_VMEM] * sets,
        scratch_shapes=[pltpu.SMEM((8, LANES), jnp.int32), pltpu.SMEM((sets, 2, genes), jnp.int32)]
        + work_space(capacity, rank_cap, sims) + [pltpu.SemaphoreType.DMA((1 + sets,))],
        compiler_params=pltpu.CompilerParams(vmem_limit_bytes=20 << 20),
        cost_estimate=pl.CostEstimate(
            flops=6 * capacity * rank_cap * sims, bytes_accessed=4 << 20, transcendentals=0
        ),
        name=f"block{block}",
    )(table, *spans, factor, normals)


def combine_kernel(classes, capacity, first, second, third, back, *refs):
    outs, stat = refs[:-1], refs[-1]
    each = outs[0].shape[0]
    total = first[...] + second[...] + third[...] + back[...]
    total = total / capacity
    for at in range(classes):
        stat[at] = total[at * each:(at + 1) * each]
    plane = lax.axis_index("genome") // QUAD
    for ahead in range(classes):
        outs[ahead][...] = stat[lax.rem(plane + ahead, classes)].astype(jnp.bfloat16)


def combine(classes, capacity, parts):
    genes, sims = parts[0].shape
    piece = jax.ShapeDtypeStruct((genes // classes, sims), jnp.bfloat16)
    return pl.pallas_call(
        functools.partial(combine_kernel, classes, capacity),
        out_shape=[piece] * classes,
        in_specs=[pl.BlockSpec(memory_space=VMEM)] * 4,
        out_specs=[pl.BlockSpec(memory_space=VMEM)] * classes,
        scratch_shapes=[pltpu.VMEM((classes, genes // classes, sims), jnp.float32)],
        compiler_params=pltpu.CompilerParams(vmem_limit_bytes=8 << 20),
        name="combine",
    )(*parts)


def member_kernel(classes, flips, genes_dev, paths, member, share):
    device = lax.axis_index("genome")
    plane, inner = device // QUAD, device % QUAD
    rows, pairs = member.shape
    genes = paths.shape[1]
    each = genes_dev // classes
    own = paths[pl.ds(inner, 1), :] - device * rows
    own = jnp.where((own >= 0) & (own < rows), own, 0).astype(jnp.float32)
    own = jnp.broadcast_to(own, (8, genes)).astype(jnp.bfloat16)
    col = lax.broadcasted_iota(jnp.int32, (genes, pairs), 1)
    gene = lax.broadcasted_iota(jnp.int32, (genes, pairs), 0)
    part = col // genes_dev
    source_in = jnp.zeros(col.shape, jnp.int32)
    for at, flip in enumerate(flips):
        source_in = jnp.where(part == at, inner ^ flip, source_in)
    behind = (col % genes_dev) // each
    source_plane = plane - behind
    source_plane = jnp.where(source_plane < 0, source_plane + classes, source_plane)
    source = source_plane * QUAD + source_in
    named = source * genes_dev + (col % each) * classes + plane
    pick = jnp.where(gene == named, 1.0, 0.0).astype(jnp.bfloat16)
    ids = jnp.dot(own, pick, preferred_element_type=jnp.float32)[0:1]
    row = lax.broadcasted_iota(jnp.int32, (rows, pairs), 0).astype(jnp.float32)
    found = jnp.where(row == ids, 1.0, 0.0)
    member[...] = found.astype(jnp.bfloat16)
    share[...] = 1.0 / jnp.sum(found, axis=1, keepdims=True)


def members(classes, flips, genes_dev, rows, paths):
    pairs = QUAD * genes_dev
    return pl.pallas_call(
        functools.partial(member_kernel, classes, flips, genes_dev),
        out_shape=[
            jax.ShapeDtypeStruct((rows, pairs), jnp.bfloat16),
            jax.ShapeDtypeStruct((rows, 1), jnp.float32),
        ],
        in_specs=[pl.BlockSpec(memory_space=VMEM)],
        out_specs=[pl.BlockSpec(memory_space=VMEM)] * 2,
        compiler_params=pltpu.CompilerParams(vmem_limit_bytes=16 << 20),
        name="members",
    )(paths)


def score_kernel(member, share, *refs):
    parts, (out, made, sems) = refs[:-3], refs[-3:]
    copies = []
    for at in range(made.shape[0]):
        cols = slice(at * COLS, (at + 1) * COLS)
        genes = jnp.concatenate([part[:, cols] for part in parts], axis=0)
        made[at] = jnp.dot(member[...], genes, preferred_element_type=jnp.float32) * share[...]
        copies.append(pltpu.make_async_copy(made.at[at], out.at[:, cols], sems.at[at]))
        copies[-1].start()
    for copy in copies:
        copy.wait()


def score(member, share, parts):
    rows, pairs = member.shape
    _, sims = parts[0].shape
    return pl.pallas_call(
        score_kernel,
        out_shape=jax.ShapeDtypeStruct((rows, sims), jnp.float32),
        in_specs=[IN_VMEM] * (2 + len(parts)),
        out_specs=ANY,
        scratch_shapes=[
            pltpu.VMEM((sims // COLS, rows, COLS), jnp.float32),
            pltpu.SemaphoreType.DMA((sims // COLS,)),
        ],
        compiler_params=pltpu.CompilerParams(vmem_limit_bytes=16 << 20),
        name="score",
    )(member, share, *parts)


def local(factor, normals, block_len, block_rank, gene_span, gene_pathways):
    block_count, capacity, _ = factor.shape
    genes = gene_span.shape[0]
    size = lax.axis_size("genome")
    classes = size // QUAD
    send = functools.partial(lax.ppermute, axis_name="genome")

    own = gene_span.T
    held = lambda x: pltpu.with_memory_space_constraint(x, pltpu.MemorySpace.HBM)
    first, *ahead_of, table = opening(classes, *map(held, (block_len, block_rank, own, factor, normals)))
    own, first = lax.optimization_barrier((own, first))
    before = send(own, perm=[(i, i + 1) for i in range(size - 1)])
    rows = PATHWAYS // size
    member, share = members(classes, (0, 2, 1, 3), genes, rows, gene_pathways.T)
    before, member, share = lax.optimization_barrier((before, member, share))
    sums = lambda block, at, spans: block_sums(block, at, block_count, classes, table, spans, *ahead_of)
    second, lent = sums(0, 0, [own, before])
    back = send(lent, perm=[(i + 1, i) for i in range(size - 1)])
    (third,) = sums(2, 1, [own])
    pieces = combine(classes, float(capacity), [first, second, third, back])

    arrived = [pieces[0]]
    for ahead in range(1, classes):
        route = [
            (c * QUAD + j, (c + ahead) % classes * QUAD + j)
            for c in range(classes)
            for j in range(QUAD)
        ]
        arrived.append(send(pieces[ahead], perm=route))
    mine = jnp.concatenate(arrived, axis=0)
    flip = lambda x, bit: send(x, perm=[(i, i ^ bit) for i in range(size)])
    across = flip(mine, 2)
    partner = flip(mine, 1)
    corner = flip(across, 1)

    return score(member, share, [mine, across, partner, corner])


def solution(mesh):
    in_specs = (
        P(("groups", "genome"), None, None),
        P(("groups", "genome"), None, None),
        P(("groups", "genome")),
        P(("groups", "genome")),
        P(("groups", "genome"), None),
        P("groups", None),
    )
    out_specs = P(("groups", "genome"), None)
    return jax.shard_map(local, mesh=mesh, in_specs=in_specs, out_specs=out_specs, check_vma=False)
```

time: 56.2 us -> 37.3 us (0.66); the launches traced: 55.6 us -> 37.5 us
  Pallas kernels: 22.9 us -> 12.4 us
  other arithmetic: 5.55 us -> 0 us
  local copies, waits for them, and re-layouts: 5.55 us -> 0.02 us
  waiting for transfers between devices: 6.07 us -> 10.4 us
  starting transfers between devices: 15.4 us -> 14.6 us
    pallas_call x4, Pallas kernels: 19.3 us -> 12 us  [the longest x2 6.29 us: block_sums(): pl.pallas_call(functools.partial(block_kernel, block, at, block_count, cl...]
    another operation x3 -> x0, other arithmetic: 5.55 us -> none  [the longest x2 4.97 us: info(): return jnp.stack([base, block_len[block], block_rank[block]])]
    slice x2 -> x0, local copies, waits for them, and re-layouts: 2.84 us -> none  [info(): return jnp.stack([base, block_len[block], block_rank[block]])]
    unnamed x15 -> x7, local copies, waits for them, and re-layouts: 2.71 us -> 0.02 us
    ppermute x3, waiting for transfers between devices: 1.13 us -> 3.61 us  [local(): arrived.append(send(pieces[ahead], perm=route))]
    pallas_call x1, Pallas kernels: 1.93 us -> 0.1 us  [combine(): pl.pallas_call(functools.partial(combine_kernel, classes, capacity), out_...]
    pallas_call x1, Pallas kernels: 1.71 us -> 0.32 us  [members(): pl.pallas_call(functools.partial(member_kernel, classes, flips, genes_dev...]
    ppermute x3, waiting for transfers between devices: 4.34 us -> 5.66 us  [local(): flip = lambda x, bit: send(x, perm=[(i, i ^ bit) for i in range(size)])]
  transfers between devices with their start and end apart: 8 -> 8, of which waited for: 3 -> 7; matrix products, arithmetic and copies ran while one was open for 16% -> 0% of each run, Pallas kernels for 20% -> 8%
where the time goes in v2:
time: 37.3 us; the launch traced here: 37.5 us
  starting transfers between devices  14.6 us (39%)
  Pallas kernels  12.4 us (33%)
  waiting for transfers between devices  10.4 us (28%)
    ppermute x3, starting transfers between devices, local(): arrived.append(send(pieces[ahead], perm=route))  10.2 us
    pallas_call x2, Pallas kernels, block_sums(): pl.pallas_call(functools.partial(block_kernel, block, at, block_count, cl...  6.29 us
    ppermute x3, waiting for transfers between devices, local(): flip = lambda x, bit: send(x, perm=[(i, i ^ bit) for i in range(size)])  5.66 us
    pallas_call x1, Pallas kernels, opening(): pl.pallas_call(functools.partial(opening_kernel, classes), out_shape=[sha...  4.49 us
    ppermute x3, waiting for transfers between devices, local(): arrived.append(send(pieces[ahead], perm=route))  3.61 us
    ppermute x1, starting transfers between devices, local(): before = send(own, perm=[(i, i + 1) for i in range(size - 1)])  2.4 us
    ppermute x1, starting transfers between devices, local(): back = send(lent, perm=[(i + 1, i) for i in range(size - 1)])  1.29 us
    pallas_call x1, Pallas kernels, score(): pl.pallas_call(score_kernel, out_shape=jax.ShapeDtypeStruct((rows, sims),...  1.25 us
  transfers between devices with their start and end apart: 8, of which 7 were waited for; matrix products, arithmetic and copies ran while one was open for 0% of the time, Pallas kernels for 8%

profile of v2, /device:TPU:0, one launch (start us, length us, event | category | flops | bytes accessed | tf_op | source)
XLA Modules:
  0.0 37.5 jit_solution(9687279654411762308)
XLA Ops:
  0.0 4.5 %opening.1 = (f32[64,1024]{1,0:T(8,128)S(1)}, bf16[2,2048,256]{2,1,0:T(8,128)(2,1)S(1)}, bf16[2,256,1024]{2,1,0:T(8,128)(2,1)S(1)}, s32[8,128]{1,0:T(8,128)S(1)}) custom-call(s32[3]{0:T(128)} %lens.1, s32[3]{0:T(128)} %ranks.1, s32[2,64]{1,0:T(2,128)} %bitcast.3, bf16[3,2048,256]{2,1,0:T(8,128)(2,1)} %factor.1, bf16[3,256,1024]{2,1,0:T(8,128)(2,1)} %normals.1), custom_call_target="tpu_custom_call" | custom-call | tf_op jit(solution)/shard_map/opening/pallas_call | solution.py:134
  4.5 0.0 copy-done.1
  4.5 2.4 %collective-permute-start = (s32[2,64]{1,0:T(2,128)S(1)}, s32[2,64]{1,0:T(2,128)S(1)}, u32[]{:S(2)}, u32[]{:S(2)}) collective-permute-start(s32[2,64]{1,0:T(2,128)S(1)} %bitcast.4), channel_id=1, source_target_pairs={{0,1},{1,2},{2,3},{3,4},{4,5},{5,6},{6,7},{7,8},{8,9},{9,10},{10,1... | collective-permute-start | bytes 1544 | tf_op jit(solution)/shard_map/ppermute | solution.py:286
  6.9 0.0 copy-done
  6.9 0.3 members.1
  7.3 0.5 %collective-permute-done.refs_1_ = s32[2,64]{1,0:T(2,128)S(1)} collective-permute-done((s32[2,64]{1,0:T(2,128)S(1)}, s32[2,64]{1,0:T(2,128)S(1)}, u32[]{:S(2)}, u32[]{:S(2)}) %collective-permute-start) | collective-permute-done | bytes 544 | tf_op jit(solution)/shard_map/ppermute | solution.py:286
  7.7 3.7 %block0.1 = (f32[64,1024]{1,0:T(8,128)S(1)}, f32[64,1024]{1,0:T(8,128)S(1)}) custom-call(s32[8,128]{1,0:T(8,128)S(1)} %get-tuple-element.29.table, s32[2,64]{1,0:T(2,128)S(1)} %bitcast.5, s32[2,64]{1,0:T(2,128)S(1)} %collective-permute-done.refs_1_, bf16[2,2048,256]{2,1,0:T(8,128)(2,1)S(1)} %get-tuple-element.31.refs_2_.refs_1_, ...), custom_call_target="tpu_custom_call" | custom-call | flops 3221225472 | bytes 4194304 | tf_op jit(solution)/shard_map/block0/pallas_call | solution.py:161
  11.4 1.3 %collective-permute-start.1 = (f32[64,1024]{1,0:T(8,128)S(1)}, f32[64,1024]{1,0:T(8,128)S(1)}, u32[]{:S(2)}, u32[]{:S(2)}) collective-permute-start(f32[64,1024]{1,0:T(8,128)S(1)} %get-tuple-element.34), channel_id=1, source_target_pairs={{1,0},{2,1},{3,2},{4,3},{5,4},{6,5},{7,6},{8,7},{9,8},{10,9},{11,1... | collective-permute-start | bytes 786440 | tf_op jit(solution)/shard_map/ppermute | solution.py:292
  12.7 2.6 %block2.1.third = f32[64,1024]{1,0:T(8,128)S(1)} custom-call(s32[8,128]{1,0:T(8,128)S(1)} %get-tuple-element.29.table, s32[2,64]{1,0:T(2,128)S(1)} %bitcast.6, bf16[2,2048,256]{2,1,0:T(8,128)(2,1)S(1)} %get-tuple-element.31.refs_2_.refs_1_, bf16[2,256,1024]{2,1,0:T(8,128)(2,1)S(1)} %get-tuple-element.32.refs_3_.refs_2_), custom_call_target="tpu_custom_call" | custom-call | flops 3221225472 | bytes 4194304 | tf_op jit(solution)/shard_map/block2/pallas_call | solution.py:161
  15.3 0.7 %collective-permute-done.1.back = f32[64,1024]{1,0:T(8,128)S(1)} collective-permute-done((f32[64,1024]{1,0:T(8,128)S(1)}, f32[64,1024]{1,0:T(8,128)S(1)}, u32[]{:S(2)}, u32[]{:S(2)}) %collective-permute-start.1) | collective-permute-done | bytes 262176 | tf_op jit(solution)/shard_map/ppermute | solution.py:292
  16.0 0.1 combine.1
  16.1 7.8 %collective-permute-start.2 = (bf16[16,1024]{1,0:T(8,128)(2,1)S(1)}, bf16[16,1024]{1,0:T(8,128)(2,1)S(1)}, u32[]{:S(2)}, u32[]{:S(2)}) collective-permute-start(bf16[16,1024]{1,0:T(8,128)(2,1)S(1)} %get-tuple-element.36), channel_id=1, source_target_pairs={{0,4},{1,5},{2,6},{3,7},{4,8},{5,9},{6,10},{7,11},{8,12},{9,13},{1... | collective-permute-start | bytes 98312 | tf_op jit(solution)/shard_map/ppermute | solution.py:303
  23.9 2.1 %collective-permute-start.3 = (bf16[16,1024]{1,0:T(8,128)(2,1)S(1)}, bf16[16,1024]{1,0:T(8,128)(2,1)S(1)}, u32[]{:S(2)}, u32[]{:S(2)}) collective-permute-start(bf16[16,1024]{1,0:T(8,128)(2,1)S(1)} %get-tuple-element.37), channel_id=1, source_target_pairs={{0,8},{1,9},{2,10},{3,11},{4,12},{5,13},{6,14},{7,15},{8,0},{9,1},... | collective-permute-start | bytes 98312 | tf_op jit(solution)/shard_map/ppermute | solution.py:303
  26.0 0.3 collective-permute-start.4
  26.3 1.1 %collective-permute-done.2 = bf16[16,1024]{1,0:T(8,128)(2,1)S(1)} collective-permute-done((bf16[16,1024]{1,0:T(8,128)(2,1)S(1)}, bf16[16,1024]{1,0:T(8,128)(2,1)S(1)}, u32[]{:S(2)}, u32[]{:S(2)}) %collective-permute-start.2) | collective-permute-done | bytes 32800 | tf_op jit(solution)/shard_map/ppermute | solution.py:303
  27.4 1.8 %collective-permute-done.3 = bf16[16,1024]{1,0:T(8,128)(2,1)S(1)} collective-permute-done((bf16[16,1024]{1,0:T(8,128)(2,1)S(1)}, bf16[16,1024]{1,0:T(8,128)(2,1)S(1)}, u32[]{:S(2)}, u32[]{:S(2)}) %collective-permute-start.3) | collective-permute-done | bytes 32800 | tf_op jit(solution)/shard_map/ppermute | solution.py:303
  29.2 0.7 %collective-permute-done.4 = bf16[16,1024]{1,0:T(8,128)(2,1)S(1)} collective-permute-done((bf16[16,1024]{1,0:T(8,128)(2,1)S(1)}, bf16[16,1024]{1,0:T(8,128)(2,1)S(1)}, u32[]{:S(2)}, u32[]{:S(2)}) %collective-permute-start.4) | collective-permute-done | bytes 32800 | tf_op jit(solution)/shard_map/ppermute | solution.py:303
  30.0 0.1 collective-permute-start.5
  30.0 0.6 %collective-permute-start.6 = (bf16[64,1024]{1,0:T(8,128)(2,1)S(1)}, bf16[64,1024]{1,0:T(8,128)(2,1)S(1)}, u32[]{:S(2)}, u32[]{:S(2)}) collective-permute-start(bf16[64,1024]{1,0:T(8,128)(2,1)S(1)} %constant_dynamic-update-slice_fusion.refs_0_), channel_id=1, source_target_pairs={{0,1},{1,0},{2,3},{3,2},{4,5},{5,4},{6,7},{7,6},{8,9},{9,8},{10,11... | collective-permute-start | bytes 393224 | tf_op jit(solution)/shard_map/ppermute | solution.py:305
  30.6 4.3 %collective-permute-done.5.refs_1_ = bf16[64,1024]{1,0:T(8,128)(2,1)S(1)} collective-permute-done((bf16[64,1024]{1,0:T(8,128)(2,1)S(1)}, bf16[64,1024]{1,0:T(8,128)(2,1)S(1)}, u32[]{:S(2)}, u32[]{:S(2)}) %collective-permute-start.5) | collective-permute-done | bytes 131104 | tf_op jit(solution)/shard_map/ppermute | solution.py:305
  34.9 0.0 collective-permute-start.7
  34.9 0.0 collective-permute-done.6.refs_2_
  34.9 1.3 %collective-permute-done.7.refs_3_ = bf16[64,1024]{1,0:T(8,128)(2,1)S(1)} collective-permute-done((bf16[64,1024]{1,0:T(8,128)(2,1)S(1)}, bf16[64,1024]{1,0:T(8,128)(2,1)S(1)}, u32[]{:S(2)}, u32[]{:S(2)}) %collective-permute-start.7) | collective-permute-done | bytes 131104 | tf_op jit(solution)/shard_map/ppermute | solution.py:305
  36.3 1.2 %score.1 = f32[256,1024]{1,0:T(8,128)} custom-call(bf16[256,256]{1,0:T(8,128)(2,1)S(1)} %get-tuple-element.26.member, f32[256,1]{1,0:T(8,128)S(1)} %get-tuple-element.27.share, bf16[64,1024]{1,0:T(8,128)(2,1)S(1)} %constant_dynamic-update-slice_fusion.refs_0_, bf16[64,1024]{1,0:T(8,128)(2,1)S(1)} %collective-permute-done.5.refs_1_, ...), custom_call_target="tpu_custom_call" | custom-call | tf_op jit(solution)/shard_map/score/pallas_call | solution.py:261
  (6 shorter events, 0.0 us)
Async XLA Ops:
  0.0 4.5 %copy-start.1 = (s32[64,2]{0,1:T(2,128)S(1)}, s32[64,2]{0,1:T(2,128)}, u32[]{:S(2)}) copy-start(s32[64,2]{0,1:T(2,128)} %param.10) | copy-start | bytes 1540
  0.0 6.9 %copy-start = (s32[1024,4]{0,1:T(4,128)S(1)}, s32[1024,4]{0,1:T(4,128)}, u32[]{:S(2)}) copy-start(s32[1024,4]{0,1:T(4,128)} %param.11) | copy-start | bytes 49156
  4.5 3.2 %collective-permute-start = (s32[2,64]{1,0:T(2,128)S(1)}, s32[2,64]{1,0:T(2,128)S(1)}, u32[]{:S(2)}, u32[]{:S(2)}) collective-permute-start(s32[2,64]{1,0:T(2,128)S(1)} %bitcast.4), channel_id=1, source_target_pairs={{0,1},{1,2},{2,3},{3,4},{4,5},{5,6},{6,7},{7,8},{8,9},{9,10},{10,1... | collective-permute-start | bytes 1544 | tf_op jit(solution)/shard_map/ppermute | solution.py:286
  11.4 4.6 %collective-permute-start.1 = (f32[64,1024]{1,0:T(8,128)S(1)}, f32[64,1024]{1,0:T(8,128)S(1)}, u32[]{:S(2)}, u32[]{:S(2)}) collective-permute-start(f32[64,1024]{1,0:T(8,128)S(1)} %get-tuple-element.34), channel_id=1, source_target_pairs={{1,0},{2,1},{3,2},{4,3},{5,4},{6,5},{7,6},{8,7},{9,8},{10,9},{11,1... | collective-permute-start | bytes 786440 | tf_op jit(solution)/shard_map/ppermute | solution.py:292
  16.1 11.3 %collective-permute-start.2 = (bf16[16,1024]{1,0:T(8,128)(2,1)S(1)}, bf16[16,1024]{1,0:T(8,128)(2,1)S(1)}, u32[]{:S(2)}, u32[]{:S(2)}) collective-permute-start(bf16[16,1024]{1,0:T(8,128)(2,1)S(1)} %get-tuple-element.36), channel_id=1, source_target_pairs={{0,4},{1,5},{2,6},{3,7},{4,8},{5,9},{6,10},{7,11},{8,12},{9,13},{1... | collective-permute-start | bytes 98312 | tf_op jit(solution)/shard_map/ppermute | solution.py:303
  23.9 5.4 %collective-permute-start.3 = (bf16[16,1024]{1,0:T(8,128)(2,1)S(1)}, bf16[16,1024]{1,0:T(8,128)(2,1)S(1)}, u32[]{:S(2)}, u32[]{:S(2)}) collective-permute-start(bf16[16,1024]{1,0:T(8,128)(2,1)S(1)} %get-tuple-element.37), channel_id=1, source_target_pairs={{0,8},{1,9},{2,10},{3,11},{4,12},{5,13},{6,14},{7,15},{8,0},{9,1},... | collective-permute-start | bytes 98312 | tf_op jit(solution)/shard_map/ppermute | solution.py:303
  26.0 3.9 %collective-permute-start.4 = (bf16[16,1024]{1,0:T(8,128)(2,1)S(1)}, bf16[16,1024]{1,0:T(8,128)(2,1)S(1)}, u32[]{:S(2)}, u32[]{:S(2)}) collective-permute-start(bf16[16,1024]{1,0:T(8,128)(2,1)S(1)} %get-tuple-element.38), channel_id=1, source_target_pairs={{0,12},{1,13},{2,14},{3,15},{4,0},{5,1},{6,2},{7,3},{8,4},{9,5},{1... | collective-permute-start | bytes 98312 | tf_op jit(solution)/shard_map/ppermute | solution.py:303
  30.0 5.0 %collective-permute-start.5 = (bf16[64,1024]{1,0:T(8,128)(2,1)S(1)}, bf16[64,1024]{1,0:T(8,128)(2,1)S(1)}, u32[]{:S(2)}, u32[]{:S(2)}) collective-permute-start(bf16[64,1024]{1,0:T(8,128)(2,1)S(1)} %constant_dynamic-update-slice_fusion.refs_0_), channel_id=1, source_target_pairs={{0,2},{1,3},{2,0},{3,1},{4,6},{5,7},{6,4},{7,5},{8,10},{9,11},{10,... | collective-permute-start | bytes 393224 | tf_op jit(solution)/shard_map/ppermute | solution.py:305
  30.0 4.9 %collective-permute-start.6 = (bf16[64,1024]{1,0:T(8,128)(2,1)S(1)}, bf16[64,1024]{1,0:T(8,128)(2,1)S(1)}, u32[]{:S(2)}, u32[]{:S(2)}) collective-permute-start(bf16[64,1024]{1,0:T(8,128)(2,1)S(1)} %constant_dynamic-update-slice_fusion.refs_0_), channel_id=1, source_target_pairs={{0,1},{1,0},{2,3},{3,2},{4,5},{5,4},{6,7},{7,6},{8,9},{9,8},{10,11... | collective-permute-start | bytes 393224 | tf_op jit(solution)/shard_map/ppermute | solution.py:305
  34.9 1.3 %collective-permute-start.7 = (bf16[64,1024]{1,0:T(8,128)(2,1)S(1)}, bf16[64,1024]{1,0:T(8,128)(2,1)S(1)}, u32[]{:S(2)}, u32[]{:S(2)}) collective-permute-start(bf16[64,1024]{1,0:T(8,128)(2,1)S(1)} %collective-permute-done.5.refs_1_), channel_id=1, source_target_pairs={{0,1},{1,0},{2,3},{3,2},{4,5},{5,4},{6,7},{7,6},{8,9},{9,8},{10,11... | collective-permute-start | bytes 393224 | tf_op jit(solution)/shard_map/ppermute | solution.py:305

commit v3 on v2

v3 whole, which is shorter than its diff:
```python
import functools

import jax
import jax.numpy as jnp
from jax import lax
from jax.experimental import pallas as pl
from jax.experimental.pallas import tpu as pltpu
from jax.sharding import PartitionSpec as P

PATHWAYS = 4096
QUAD = 4
CHUNK = 1024
COLS = 256
LANES = 128
VMEM = pltpu.MemorySpace.VMEM
SMEM = pltpu.MemorySpace.SMEM


def reduce_parts(parts, side, out, first):
    for tile in range(parts.shape[1]):
        total = parts[side, tile, pl.ds(0, 8, stride=8), :]
        for sub in range(1, 8):
            total = total + parts[side, tile, pl.ds(sub, 8, stride=8), :]
        out[first:first + 8, tile * LANES:(tile + 1) * LANES] = total


def class_major(place, each, classes):
    return place % each * classes + place // each


def mask_ranks(normals, rank, vectors):
    rank_cap, sims = normals.shape
    row = lax.broadcasted_iota(jnp.int32, (rank_cap, LANES), 0)
    keep = jnp.where(row < rank, 1.0, 0.0).astype(jnp.bfloat16)
    for tile in range(sims // LANES):
        cols = slice(tile * LANES, (tile + 1) * LANES)
        vectors[:, cols] = normals[:, cols] * keep


def running_sums(rows, vectors, prefix, start):
    count, sims = rows.shape[0], vectors.shape[1]
    for col in range(0, sims, COLS):
        coloured = jnp.dot(rows, vectors[:, col:col + COLS], preferred_element_type=jnp.float32)
        square = coloured * coloured
        for part in range(COLS // LANES):
            tile = col // LANES + part
            lane = slice(part * LANES, (part + 1) * LANES)
            run = prefix[tile, start:start + 8, :]
            for at in range(0, count, 32):
                inner = None
                for row in range(at, at + 32, 8):
                    inner = square[row:row + 8, lane] if inner is None else inner + square[row:row + 8, lane]
                    prefix[tile, start + row + 8:start + row + 16, :] = run + inner
                run = run + inner


def opening_kernel(lens, ranks, factor, normals, prefix, next_factor, next_normals, table,
                   lens_in, ranks_in, factor_in, normals_in, vectors, sems):
    block_count, capacity, _ = factor.shape
    chunks = capacity // CHUNK
    copies = [
        pltpu.make_async_copy(source, target, sems.at[at])
        for at, (source, target) in enumerate(
            [(ranks, ranks_in), (lens, lens_in), (normals.at[0], normals_in)]
            + [(factor.at[0, c * CHUNK:(c + 1) * CHUNK], factor_in.at[c * CHUNK:(c + 1) * CHUNK]) for c in range(chunks)]
            + [(normals.at[k], next_normals.at[k - 1]) for k in range(1, block_count)]
            + [(factor.at[k], next_factor.at[k - 1]) for k in range(1, block_count)]
        )
    ]
    for copy in copies[:3 + chunks]:
        copy.start()
    for tile in range(prefix.shape[0]):
        prefix[tile, 0:8, :] = jnp.zeros((8, LANES), jnp.float32)
    for copy in copies[:3]:
        copy.wait()
    for block in range(block_count):
        table[block:block + 1, :] = jnp.full((1, LANES), ranks_in[block], jnp.int32)
        table[block_count + block:block_count + block + 1, :] = jnp.full((1, LANES), lens_in[block], jnp.int32)
    mask_ranks(normals_in, ranks_in[0], vectors)
    for copy in copies[3 + chunks:]:
        copy.start()
    for chunk in range(chunks):
        copies[3 + chunk].wait()

        @pl.when(chunk * CHUNK < lens_in[0])
        def _():
            rows = slice(chunk * CHUNK, (chunk + 1) * CHUNK)
            running_sums(factor_in[rows, :], vectors, prefix, chunk * CHUNK)
    for copy in copies[3 + chunks:]:
        copy.wait()


def lending_kernel(block_count, classes, table, spans, prefix, out, table_in, spans_in, parts, sems):
    copies = [
        pltpu.make_async_copy(table, table_in, sems.at[0]),
        pltpu.make_async_copy(spans, spans_in, sems.at[1]),
    ]
    for copy in copies:
        copy.start()
    for copy in copies:
        copy.wait()
    genes = spans.shape[1]
    capacity = prefix.shape[1] // block_count - 8
    base = lax.axis_index("genome") * block_count * capacity
    length = table_in[block_count, 0]
    for first in range(0, genes, 8):
        side = first // 8 % parts.shape[0]
        for slot in range(8):
            gene = class_major(first + slot, genes // classes, classes)
            upper = jnp.clip(spans_in[1, gene] - base, 0, length)
            for tile in range(prefix.shape[0]):
                parts[side, tile, slot * 8:slot * 8 + 8, :] = prefix[tile, pl.ds(upper, 8), :]
        reduce_parts(parts, side, out, first)


def closing_kernel(classes, table, spans, lent, factor, normals, old_prefix, prefix, out,
                   table_in, spans_in, vectors, parts, sems):
    del lent, old_prefix
    block_count, capacity = factor.shape[0] + 1, factor.shape[1]
    copies = [
        pltpu.make_async_copy(table, table_in, sems.at[0]),
        pltpu.make_async_copy(spans, spans_in, sems.at[1]),
    ]
    for copy in copies:
        copy.start()
    stride = capacity + 8
    for block in range(1, block_count):
        mask_ranks(normals.at[block - 1], table[block:block + 1, :], vectors)
        if block == 1:
            for copy in copies:
                copy.wait()
            length = [table_in[block_count + k, 0] for k in range(block_count)]
        for tile in range(prefix.shape[0]):
            carry = prefix[tile, pl.ds((block - 1) * stride + length[block - 1], 8), :]
            prefix[tile, block * stride:block * stride + 8, :] = carry
        for chunk in range(capacity // CHUNK):
            @pl.when(chunk * CHUNK < length[block])
            def _():
                rows = slice(chunk * CHUNK, (chunk + 1) * CHUNK)
                running_sums(factor[block - 1, rows, :], vectors, prefix, block * stride + chunk * CHUNK)

    genes = spans.shape[1]
    base = lax.axis_index("genome") * block_count * capacity

    def place(slot):
        slot = slot - base
        at = jnp.minimum(slot, length[0])
        for block in range(1, block_count):
            here = jnp.minimum(slot - block * capacity, length[block]) + block * stride
            at = jnp.where(slot >= block * capacity, here, at)
        return at

    for first in range(0, genes, 8):
        side = first // 8 % parts.shape[0]
        for slot in range(8):
            gene = class_major(first + slot, genes // classes, classes)
            lower, upper = place(spans_in[0, gene]), place(spans_in[1, gene])
            for tile in range(prefix.shape[0]):
                parts[side, tile, slot * 8:slot * 8 + 8, :] = (
                    prefix[tile, pl.ds(upper, 8), :] - prefix[tile, pl.ds(lower, 8), :]
                )
        reduce_parts(parts, side, out, first)


ANY, IN_VMEM = pl.BlockSpec(memory_space=pl.ANY), pl.BlockSpec(memory_space=VMEM)
IN_HBM = pl.BlockSpec(memory_space=pltpu.MemorySpace.HBM)


def opening(lens, ranks, factor, normals):
    block_count, capacity, rank_cap = factor.shape
    sims = normals.shape[2]
    shape = jax.ShapeDtypeStruct
    return pl.pallas_call(
        opening_kernel,
        out_shape=[
            shape((sims // LANES, block_count * (capacity + 8), LANES), jnp.float32),
            shape((block_count - 1, capacity, rank_cap), factor.dtype),
            shape((block_count - 1, rank_cap, sims), normals.dtype),
            shape((8, LANES), jnp.int32),
        ],
        in_specs=[IN_HBM] * 4,
        out_specs=[IN_VMEM] * 4,
        scratch_shapes=[
            pltpu.SMEM((block_count,), jnp.int32),
            pltpu.SMEM((block_count,), jnp.int32),
            pltpu.VMEM((capacity, rank_cap), factor.dtype),
            pltpu.VMEM((rank_cap, sims), normals.dtype),
            pltpu.VMEM((rank_cap, sims), jnp.bfloat16),
            pltpu.SemaphoreType.DMA((1 + 2 * block_count + capacity // CHUNK,)),
        ],
        compiler_params=pltpu.CompilerParams(vmem_limit_bytes=8 << 20),
        name="opening",
    )(lens, ranks, factor, normals)


def lending(block_count, classes, table, spans, prefix):
    genes = spans.shape[1]
    tiles = prefix.shape[0]
    return pl.pallas_call(
        functools.partial(lending_kernel, block_count, classes),
        out_shape=jax.ShapeDtypeStruct((genes, tiles * LANES), jnp.float32),
        in_specs=[ANY, ANY, IN_VMEM],
        out_specs=IN_VMEM,
        scratch_shapes=[
            pltpu.SMEM((8, LANES), jnp.int32),
            pltpu.SMEM((2, genes), jnp.int32),
            pltpu.VMEM((2, tiles, 64, LANES), jnp.float32),
            pltpu.SemaphoreType.DMA((2,)),
        ],
        compiler_params=pltpu.CompilerParams(vmem_limit_bytes=4 << 20),
        name="lending",
    )(table, spans, prefix)


def closing(classes, table, spans, lent, factor, normals, prefix):
    genes = spans.shape[1]
    tiles = prefix.shape[0]
    _, capacity, rank_cap = factor.shape
    sims = tiles * LANES
    return pl.pallas_call(
        functools.partial(closing_kernel, classes),
        out_shape=[
            jax.ShapeDtypeStruct(prefix.shape, jnp.float32),
            jax.ShapeDtypeStruct((genes, sims), jnp.float32),
        ],
        in_specs=[IN_VMEM, ANY, ANY] + [IN_VMEM] * 3,
        out_specs=[IN_VMEM] * 2,
        input_output_aliases={5: 0},
        scratch_shapes=[
            pltpu.SMEM((8, LANES), jnp.int32),
            pltpu.SMEM((2, genes), jnp.int32),
            pltpu.VMEM((rank_cap, sims), jnp.bfloat16),
            pltpu.VMEM((2, tiles, 64, LANES), jnp.float32),
            pltpu.SemaphoreType.DMA((2,)),
        ],
        compiler_params=pltpu.CompilerParams(vmem_limit_bytes=8 << 20),
        cost_estimate=pl.CostEstimate(
            flops=6 * capacity * rank_cap * sims, bytes_accessed=16 << 20, transcendentals=0
        ),
        name="closing",
    )(table, spans, lent, factor, normals, prefix)


def combine_kernel(classes, capacity, held, back, *refs):
    outs, stat = refs[:-1], refs[-1]
    each = outs[0].shape[0]
    total = (held[...] + back[...]) / capacity
    for at in range(classes):
        stat[at] = total[at * each:(at + 1) * each]
    plane = lax.axis_index("genome") // QUAD
    for apart in range(classes):
        outs[apart][...] = stat[plane ^ apart].astype(jnp.bfloat16)


def combine(classes, capacity, parts):
    genes, sims = parts[0].shape
    piece = jax.ShapeDtypeStruct((genes // classes, sims), jnp.bfloat16)
    return pl.pallas_call(
        functools.partial(combine_kernel, classes, capacity),
        out_shape=[piece] * classes,
        in_specs=[pl.BlockSpec(memory_space=VMEM)] * 2,
        out_specs=[pl.BlockSpec(memory_space=VMEM)] * classes,
        scratch_shapes=[pltpu.VMEM((classes, genes // classes, sims), jnp.float32)],
        compiler_params=pltpu.CompilerParams(vmem_limit_bytes=8 << 20),
        name="combine",
    )(*parts)


def member_kernel(classes, flips, genes_dev, paths, member, share):
    device = lax.axis_index("genome")
    plane, inner = device // QUAD, device % QUAD
    rows, pairs = member.shape
    genes = paths.shape[1]
    each = genes_dev // classes
    own = paths[pl.ds(inner, 1), :] - device * rows
    own = jnp.where((own >= 0) & (own < rows), own, 0).astype(jnp.float32)
    own = jnp.broadcast_to(own, (8, genes)).astype(jnp.bfloat16)
    col = lax.broadcasted_iota(jnp.int32, (genes, pairs), 1)
    gene = lax.broadcasted_iota(jnp.int32, (genes, pairs), 0)
    part = col // genes_dev
    source_in = jnp.zeros(col.shape, jnp.int32)
    for at, flip in enumerate(flips):
        source_in = jnp.where(part == at, inner ^ flip, source_in)
    source_plane = plane ^ ((col % genes_dev) // each)
    source = source_plane * QUAD + source_in
    named = source * genes_dev + (col % each) * classes + plane
    pick = jnp.where(gene == named, 1.0, 0.0).astype(jnp.bfloat16)
    ids = jnp.dot(own, pick, preferred_element_type=jnp.float32)[0:1]
    row = lax.broadcasted_iota(jnp.int32, (rows, pairs), 0).astype(jnp.float32)
    found = jnp.where(row == ids, 1.0, 0.0)
    member[...] = found.astype(jnp.bfloat16)
    share[...] = 1.0 / jnp.sum(found, axis=1, keepdims=True)


def members(classes, flips, genes_dev, rows, paths):
    pairs = QUAD * genes_dev
    return pl.pallas_call(
        functools.partial(member_kernel, classes, flips, genes_dev),
        out_shape=[
            jax.ShapeDtypeStruct((rows, pairs), jnp.bfloat16),
            jax.ShapeDtypeStruct((rows, 1), jnp.float32),
        ],
        in_specs=[pl.BlockSpec(memory_space=VMEM)],
        out_specs=[pl.BlockSpec(memory_space=VMEM)] * 2,
        compiler_params=pltpu.CompilerParams(vmem_limit_bytes=16 << 20),
        name="members",
    )(paths)


def score_kernel(member, share, *refs):
    parts, (out, made, sems) = refs[:-3], refs[-3:]
    copies = []
    for at in range(made.shape[0]):
        cols = slice(at * COLS, (at + 1) * COLS)
        genes = jnp.concatenate([part[:, cols] for part in parts], axis=0)
        made[at] = jnp.dot(member[...], genes, preferred_element_type=jnp.float32) * share[...]
        copies.append(pltpu.make_async_copy(made.at[at], out.at[:, cols], sems.at[at]))
        copies[-1].start()
    for copy in copies:
        copy.wait()


def score(member, share, parts):
    rows, pairs = member.shape
    _, sims = parts[0].shape
    return pl.pallas_call(
        score_kernel,
        out_shape=jax.ShapeDtypeStruct((rows, sims), jnp.float32),
        in_specs=[IN_VMEM] * (2 + len(parts)),
        out_specs=ANY,
        scratch_shapes=[
            pltpu.VMEM((sims // COLS, rows, COLS), jnp.float32),
            pltpu.SemaphoreType.DMA((sims // COLS,)),
        ],
        compiler_params=pltpu.CompilerParams(vmem_limit_bytes=16 << 20),
        name="score",
    )(member, share, *parts)


def local(factor, normals, block_len, block_rank, gene_span, gene_pathways):
    block_count, capacity, _ = factor.shape
    genes = gene_span.shape[0]
    size = lax.axis_size("genome")
    classes = size // QUAD
    send = functools.partial(lax.ppermute, axis_name="genome")

    own = gene_span.T
    before = send(own, perm=[(i, i + 1) for i in range(size - 1)])
    held = lambda x: pltpu.with_memory_space_constraint(x, pltpu.MemorySpace.HBM)
    prefix, next_factor, next_normals, table = opening(*map(held, (block_len, block_rank, factor, normals)))
    lent = lending(block_count, classes, table, before, prefix)
    back = send(lent, perm=[(i + 1, i) for i in range(size - 1)])
    _, sums = closing(classes, table, own, lent, next_factor, next_normals, prefix)
    paths, sums = lax.optimization_barrier((gene_pathways.T, sums))
    rows = PATHWAYS // size
    member, share = members(classes, (0, 2, 1, 3), genes, rows, paths)
    back, member, share = lax.optimization_barrier((back, member, share))
    pieces = combine(classes, float(capacity), [sums, back])

    flip = lambda x, bits: send(x, perm=[(i, i ^ bits) for i in range(size)])
    arrived = [flip(pieces[apart], apart * QUAD) for apart in reversed(range(1, classes))]
    arrived = [pieces[0]] + arrived[::-1]
    mine = jnp.concatenate(arrived, axis=0)
    across = flip(mine, 2)
    partner = flip(mine, 1)
    corner = flip(across, 1)

    return score(member, share, [mine, across, partner, corner])


def solution(mesh):
    in_specs = (
        P(("groups", "genome"), None, None),
        P(("groups", "genome"), None, None),
        P(("groups", "genome")),
        P(("groups", "genome")),
        P(("groups", "genome"), None),
        P("groups", None),
    )
    out_specs = P(("groups", "genome"), None)
    return jax.shard_map(local, mesh=mesh, in_specs=in_specs, out_specs=out_specs, check_vma=False)
```

time: 37.3 us -> 34.4 us (0.922); the launches traced: 37.5 us -> 33.9 us
  Pallas kernels: 12.4 us -> 9.54 us
  starting transfers between devices: 14.6 us -> 14 us
    pallas_call x3, Pallas kernels: 10.8 us -> 7.92 us  [the longest x1 3.78 us: closing(): pl.pallas_call(functools.partial(closing_kernel, classes), out_shape=[jax...]
    ppermute x6, waiting for transfers between devices: 9.27 us -> 10.1 us  [local(): flip = lambda x, bits: send(x, perm=[(i, i ^ bits) for i in range(size)])]
    ppermute x6, starting transfers between devices: 10.9 us -> 10.3 us  [local(): flip = lambda x, bits: send(x, perm=[(i, i ^ bits) for i in range(size)])]
    ppermute x1, waiting for transfers between devices: 0.67 us -> 0.11 us  [local(): back = send(lent, perm=[(i + 1, i) for i in range(size - 1)])]
    ppermute x1, waiting for transfers between devices: 0.47 us -> 0.01 us  [local(): before = send(own, perm=[(i, i + 1) for i in range(size - 1)])]
  transfers between devices with their start and end apart: 8 -> 8, of which waited for: 7 -> 5; matrix products, arithmetic and copies ran while one was open for 0% -> 0% of each run, Pallas kernels for 8% -> 21%
where the time goes in v3:
time: 34.4 us; the launch traced here: 33.9 us
  starting transfers between devices  14 us (41%)
  waiting for transfers between devices  10.2 us (30%)
  Pallas kernels  9.54 us (28%)
    ppermute x6, starting transfers between devices, local(): flip = lambda x, bits: send(x, perm=[(i, i ^ bits) for i in range(size)])  10.3 us
    ppermute x6, waiting for transfers between devices, local(): flip = lambda x, bits: send(x, perm=[(i, i ^ bits) for i in range(size)])  10.1 us
    pallas_call x1, Pallas kernels, closing(): pl.pallas_call(functools.partial(closing_kernel, classes), out_shape=[jax...  3.78 us
    pallas_call x1, Pallas kernels, opening(): pl.pallas_call(opening_kernel, out_shape=[shape((sims // LANES, block_cou...  3.06 us
    ppermute x1, starting transfers between devices, local(): before = send(own, perm=[(i, i + 1) for i in range(size - 1)])  2.39 us
    ppermute x1, starting transfers between devices, local(): back = send(lent, perm=[(i + 1, i) for i in range(size - 1)])  1.29 us
    pallas_call x1, Pallas kernels, score(): pl.pallas_call(score_kernel, out_shape=jax.ShapeDtypeStruct((rows, sims),...  1.25 us
    pallas_call x1, Pallas kernels, lending(): pl.pallas_call(functools.partial(lending_kernel, block_count, classes), o...  1.09 us
  transfers between devices with their start and end apart: 8, of which 5 were waited for; matrix products, arithmetic and copies ran while one was open for 0% of the time, Pallas kernels for 21%

profile of v3, /device:TPU:0, one launch (start us, length us, event | category | flops | bytes accessed | tf_op | source)
XLA Modules:
  0.0 33.9 jit_solution(8679403402032343832)
XLA Ops:
  0.0 2.4 %collective-permute-start = (s32[2,64]{1,0:T(2,128)}, s32[2,64]{1,0:T(2,128)S(1)}, u32[]{:S(2)}, u32[]{:S(2)}) collective-permute-start(s32[2,64]{1,0:T(2,128)} %bitcast.3), channel_id=1, source_target_pairs={{0,1},{1,2},{2,3},{3,4},{4,5},{5,6},{6,7},{7,8},{8,9},{9,10},{10,1... | collective-permute-start | bytes 1544 | tf_op jit(solution)/shard_map/ppermute | solution.py:348
  2.4 3.1 %opening.1 = (f32[8,6168,128]{2,1,0:T(8,128)S(1)}, bf16[2,2048,256]{2,1,0:T(8,128)(2,1)S(1)}, bf16[2,256,1024]{2,1,0:T(8,128)(2,1)S(1)}, s32[8,128]{1,0:T(8,128)S(1)}) custom-call(s32[3]{0:T(128)} %lens.1, s32[3]{0:T(128)} %ranks.1, bf16[3,2048,256]{2,1,0:T(8,128)(2,1)} %factor.1, bf16[3,256,1024]{2,1,0:T(8,128)(2,1)} %normals.1), custom_call_target="tpu_custom_call" | custom-call | tf_op jit(solution)/shard_map/opening/pallas_call | solution.py:173
  5.5 0.0 collective-permute-done.spans
  5.5 0.0 copy-start.1
  5.5 1.1 %lending.1.lent = f32[64,1024]{1,0:T(8,128)S(1)} custom-call(s32[8,128]{1,0:T(8,128)S(1)} %get-tuple-element.21.table, s32[2,64]{1,0:T(2,128)S(1)} %collective-permute-done.spans, f32[8,6168,128]{2,1,0:T(8,128)S(1)} %get-tuple-element.22.prefix.old_prefix), custom_call_target="tpu_custom_call" | custom-call | tf_op jit(solution)/shard_map/lending/pallas_call | solution.py:199
  6.6 1.3 %collective-permute-start.1 = (f32[64,1024]{1,0:T(8,128)S(1)}, f32[64,1024]{1,0:T(8,128)S(1)}, u32[]{:S(2)}, u32[]{:S(2)}) collective-permute-start(f32[64,1024]{1,0:T(8,128)S(1)} %lending.1.lent), channel_id=1, source_target_pairs={{1,0},{2,1},{3,2},{4,3},{5,4},{6,5},{7,6},{8,7},{9,8},{10,9},{11,1... | collective-permute-start | bytes 786440 | tf_op jit(solution)/shard_map/ppermute | solution.py:352
  7.9 0.0 copy-done.1
  7.9 0.0 copy-start
  7.9 3.8 %closing.1 = (f32[8,6168,128]{2,1,0:T(8,128)S(1)}, f32[64,1024]{1,0:T(8,128)S(1)}) custom-call(s32[8,128]{1,0:T(8,128)S(1)} %get-tuple-element.21.table, s32[2,64]{1,0:T(2,128)S(1)} %bitcast.4, f32[64,1024]{1,0:T(8,128)S(1)} %lending.1.lent, bf16[2,2048,256]{2,1,0:T(8,128)(2,1)S(1)} %get-tuple-element.23.factor, ...), custom_call_target="tpu_custom_call", output_to_operand_aliasing={{0}: (5, {})} | custom-call | flops 3221225472 | bytes 16777216 | tf_op jit(solution)/shard_map/closing/pallas_call | solution.py:220
  11.7 0.3 members.1
  12.0 0.1 collective-permute-done.1.back
  12.2 6.5 %collective-permute-start.2 = (bf16[16,1024]{1,0:T(8,128)(2,1)S(1)}, bf16[16,1024]{1,0:T(8,128)(2,1)S(1)}, u32[]{:S(2)}, u32[]{:S(2)}) collective-permute-start(bf16[16,1024]{1,0:T(8,128)(2,1)S(1)} %get-tuple-element.34), channel_id=1, source_target_pairs={{0,4},{1,5},{2,6},{3,7},{4,0},{5,1},{6,2},{7,3},{8,12},{9,13},{10,... | collective-permute-start | bytes 98312 | tf_op jit(solution)/shard_map/ppermute | solution.py:360
  18.7 1.9 %collective-permute-start.3 = (bf16[16,1024]{1,0:T(8,128)(2,1)S(1)}, bf16[16,1024]{1,0:T(8,128)(2,1)S(1)}, u32[]{:S(2)}, u32[]{:S(2)}) collective-permute-start(bf16[16,1024]{1,0:T(8,128)(2,1)S(1)} %get-tuple-element.35), channel_id=1, source_target_pairs={{0,8},{1,9},{2,10},{3,11},{4,12},{5,13},{6,14},{7,15},{8,0},{9,1},... | collective-permute-start | bytes 98312 | tf_op jit(solution)/shard_map/ppermute | solution.py:360
  20.6 0.6 %collective-permute-start.4 = (bf16[16,1024]{1,0:T(8,128)(2,1)S(1)}, bf16[16,1024]{1,0:T(8,128)(2,1)S(1)}, u32[]{:S(2)}, u32[]{:S(2)}) collective-permute-start(bf16[16,1024]{1,0:T(8,128)(2,1)S(1)} %get-tuple-element.36), channel_id=1, source_target_pairs={{0,12},{1,13},{2,14},{3,15},{4,8},{5,9},{6,10},{7,11},{8,4},{9,5},... | collective-permute-start | bytes 98312 | tf_op jit(solution)/shard_map/ppermute | solution.py:360
  21.1 0.0 collective-permute-done.2
  21.1 2.7 %collective-permute-done.3 = bf16[16,1024]{1,0:T(8,128)(2,1)S(1)} collective-permute-done((bf16[16,1024]{1,0:T(8,128)(2,1)S(1)}, bf16[16,1024]{1,0:T(8,128)(2,1)S(1)}, u32[]{:S(2)}, u32[]{:S(2)}) %collective-permute-start.3) | collective-permute-done | bytes 32800 | tf_op jit(solution)/shard_map/ppermute | solution.py:360
  23.8 2.5 %collective-permute-done.4 = bf16[16,1024]{1,0:T(8,128)(2,1)S(1)} collective-permute-done((bf16[16,1024]{1,0:T(8,128)(2,1)S(1)}, bf16[16,1024]{1,0:T(8,128)(2,1)S(1)}, u32[]{:S(2)}, u32[]{:S(2)}) %collective-permute-start.4) | collective-permute-done | bytes 32800 | tf_op jit(solution)/shard_map/ppermute | solution.py:360
  26.3 1.3 %collective-permute-start.5 = (bf16[64,1024]{1,0:T(8,128)(2,1)S(1)}, bf16[64,1024]{1,0:T(8,128)(2,1)S(1)}, u32[]{:S(2)}, u32[]{:S(2)}) collective-permute-start(bf16[64,1024]{1,0:T(8,128)(2,1)S(1)} %constant_dynamic-update-slice_fusion.refs_0_), channel_id=1, source_target_pairs={{0,2},{1,3},{2,0},{3,1},{4,6},{5,7},{6,4},{7,5},{8,10},{9,11},{10,... | collective-permute-start | bytes 393224 | tf_op jit(solution)/shard_map/ppermute | solution.py:360
  27.6 0.0 collective-permute-start.6
  27.6 3.6 %collective-permute-done.5.refs_1_ = bf16[64,1024]{1,0:T(8,128)(2,1)S(1)} collective-permute-done((bf16[64,1024]{1,0:T(8,128)(2,1)S(1)}, bf16[64,1024]{1,0:T(8,128)(2,1)S(1)}, u32[]{:S(2)}, u32[]{:S(2)}) %collective-permute-start.5) | collective-permute-done | bytes 131104 | tf_op jit(solution)/shard_map/ppermute | solution.py:360
  31.3 0.0 collective-permute-start.7
  31.3 0.0 collective-permute-done.6.refs_2_
  31.3 1.3 %collective-permute-done.7.refs_3_ = bf16[64,1024]{1,0:T(8,128)(2,1)S(1)} collective-permute-done((bf16[64,1024]{1,0:T(8,128)(2,1)S(1)}, bf16[64,1024]{1,0:T(8,128)(2,1)S(1)}, u32[]{:S(2)}, u32[]{:S(2)}) %collective-permute-start.7) | collective-permute-done | bytes 131104 | tf_op jit(solution)/shard_map/ppermute | solution.py:360
  32.6 1.2 %score.1 = f32[256,1024]{1,0:T(8,128)} custom-call(bf16[256,256]{1,0:T(8,128)(2,1)S(1)} %get-tuple-element.29.member, f32[256,1]{1,0:T(8,128)S(1)} %get-tuple-element.30.share, bf16[64,1024]{1,0:T(8,128)(2,1)S(1)} %constant_dynamic-update-slice_fusion.refs_0_, bf16[64,1024]{1,0:T(8,128)(2,1)S(1)} %collective-permute-done.5.refs_1_, ...), custom_call_target="tpu_custom_call" | custom-call | tf_op jit(solution)/shard_map/score/pallas_call | solution.py:326
  (6 shorter events, 0.1 us)
Async XLA Ops:
  0.0 5.5 %collective-permute-start = (s32[2,64]{1,0:T(2,128)}, s32[2,64]{1,0:T(2,128)S(1)}, u32[]{:S(2)}, u32[]{:S(2)}) collective-permute-start(s32[2,64]{1,0:T(2,128)} %bitcast.3), channel_id=1, source_target_pairs={{0,1},{1,2},{2,3},{3,4},{4,5},{5,6},{6,7},{7,8},{8,9},{9,10},{10,1... | collective-permute-start | bytes 1544 | tf_op jit(solution)/shard_map/ppermute | solution.py:348
  5.5 2.4 %copy-start.1 = (s32[64,2]{0,1:T(2,128)S(1)}, s32[64,2]{0,1:T(2,128)}, u32[]{:S(2)}) copy-start(s32[64,2]{0,1:T(2,128)} %param.10) | copy-start | bytes 1540
  6.6 5.6 %collective-permute-start.1 = (f32[64,1024]{1,0:T(8,128)S(1)}, f32[64,1024]{1,0:T(8,128)S(1)}, u32[]{:S(2)}, u32[]{:S(2)}) collective-permute-start(f32[64,1024]{1,0:T(8,128)S(1)} %lending.1.lent), channel_id=1, source_target_pairs={{1,0},{2,1},{3,2},{4,3},{5,4},{6,5},{7,6},{8,7},{9,8},{10,9},{11,1... | collective-permute-start | bytes 786440 | tf_op jit(solution)/shard_map/ppermute | solution.py:352
  7.9 3.8 %copy-start = (s32[1024,4]{0,1:T(4,128)S(1)}, s32[1024,4]{0,1:T(4,128)}, u32[]{:S(2)}) copy-start(s32[1024,4]{0,1:T(4,128)} %param.11) | copy-start | bytes 49156
  12.2 9.0 %collective-permute-start.2 = (bf16[16,1024]{1,0:T(8,128)(2,1)S(1)}, bf16[16,1024]{1,0:T(8,128)(2,1)S(1)}, u32[]{:S(2)}, u32[]{:S(2)}) collective-permute-start(bf16[16,1024]{1,0:T(8,128)(2,1)S(1)} %get-tuple-element.34), channel_id=1, source_target_pairs={{0,4},{1,5},{2,6},{3,7},{4,0},{5,1},{6,2},{7,3},{8,12},{9,13},{10,... | collective-permute-start | bytes 98312 | tf_op jit(solution)/shard_map/ppermute | solution.py:360
  18.7 5.1 %collective-permute-start.3 = (bf16[16,1024]{1,0:T(8,128)(2,1)S(1)}, bf16[16,1024]{1,0:T(8,128)(2,1)S(1)}, u32[]{:S(2)}, u32[]{:S(2)}) collective-permute-start(bf16[16,1024]{1,0:T(8,128)(2,1)S(1)} %get-tuple-element.35), channel_id=1, source_target_pairs={{0,8},{1,9},{2,10},{3,11},{4,12},{5,13},{6,14},{7,15},{8,0},{9,1},... | collective-permute-start | bytes 98312 | tf_op jit(solution)/shard_map/ppermute | solution.py:360
  20.6 5.7 %collective-permute-start.4 = (bf16[16,1024]{1,0:T(8,128)(2,1)S(1)}, bf16[16,1024]{1,0:T(8,128)(2,1)S(1)}, u32[]{:S(2)}, u32[]{:S(2)}) collective-permute-start(bf16[16,1024]{1,0:T(8,128)(2,1)S(1)} %get-tuple-element.36), channel_id=1, source_target_pairs={{0,12},{1,13},{2,14},{3,15},{4,8},{5,9},{6,10},{7,11},{8,4},{9,5},... | collective-permute-start | bytes 98312 | tf_op jit(solution)/shard_map/ppermute | solution.py:360
  26.3 5.0 %collective-permute-start.5 = (bf16[64,1024]{1,0:T(8,128)(2,1)S(1)}, bf16[64,1024]{1,0:T(8,128)(2,1)S(1)}, u32[]{:S(2)}, u32[]{:S(2)}) collective-permute-start(bf16[64,1024]{1,0:T(8,128)(2,1)S(1)} %constant_dynamic-update-slice_fusion.refs_0_), channel_id=1, source_target_pairs={{0,2},{1,3},{2,0},{3,1},{4,6},{5,7},{6,4},{7,5},{8,10},{9,11},{10,... | collective-permute-start | bytes 393224 | tf_op jit(solution)/shard_map/ppermute | solution.py:360
  27.6 3.6 %collective-permute-start.6 = (bf16[64,1024]{1,0:T(8,128)(2,1)S(1)}, bf16[64,1024]{1,0:T(8,128)(2,1)S(1)}, u32[]{:S(2)}, u32[]{:S(2)}) collective-permute-start(bf16[64,1024]{1,0:T(8,128)(2,1)S(1)} %constant_dynamic-update-slice_fusion.refs_0_), channel_id=1, source_target_pairs={{0,1},{1,0},{2,3},{3,2},{4,5},{5,4},{6,7},{7,6},{8,9},{9,8},{10,11... | collective-permute-start | bytes 393224 | tf_op jit(solution)/shard_map/ppermute | solution.py:360
  31.3 1.3 %collective-permute-start.7 = (bf16[64,1024]{1,0:T(8,128)(2,1)S(1)}, bf16[64,1024]{1,0:T(8,128)(2,1)S(1)}, u32[]{:S(2)}, u32[]{:S(2)}) collective-permute-start(bf16[64,1024]{1,0:T(8,128)(2,1)S(1)} %collective-permute-done.5.refs_1_), channel_id=1, source_target_pairs={{0,1},{1,0},{2,3},{3,2},{4,5},{5,4},{6,7},{7,6},{8,9},{9,8},{10,11... | collective-permute-start | bytes 393224 | tf_op jit(solution)/shard_map/ppermute | solution.py:360

commit v4 on v3

--- a/solution.py
+++ b/solution.py
@@ -7,13 +7,13 @@
 from jax.experimental.pallas import tpu as pltpu
 from jax.sharding import PartitionSpec as P
 
+
 PATHWAYS = 4096
 QUAD = 4
 CHUNK = 1024
 COLS = 256
 LANES = 128
 VMEM = pltpu.MemorySpace.VMEM
-SMEM = pltpu.MemorySpace.SMEM
 
 
 def reduce_parts(parts, side, out, first):
@@ -105,12 +105,22 @@
     length = table_in[block_count, 0]
     for first in range(0, genes, 8):
         side = first // 8 % parts.shape[0]
+        ends = []
         for slot in range(8):
             gene = class_major(first + slot, genes // classes, classes)
-            upper = jnp.clip(spans_in[1, gene] - base, 0, length)
-            for tile in range(prefix.shape[0]):
-                parts[side, tile, slot * 8:slot * 8 + 8, :] = prefix[tile, pl.ds(upper, 8), :]
-        reduce_parts(parts, side, out, first)
+            ends.append(jnp.clip(spans_in[1, gene] - base, 0, length))
+        reach = functools.reduce(jnp.maximum, ends)
+
+        @pl.when(reach > 0)
+        def _():
+            for slot, end in enumerate(ends):
+                for tile in range(prefix.shape[0]):
+                    parts[side, tile, slot * 8:slot * 8 + 8, :] = prefix[tile, pl.ds(end, 8), :]
+            reduce_parts(parts, side, out, first)
+
+        @pl.when(reach == 0)
+        def _():
+            out[first:first + 8, :] = jnp.zeros((8, out.shape[1]), jnp.float32)
 
 
 def closing_kernel(classes, table, spans, lent, factor, normals, old_prefix, prefix, out,
@@ -281,7 +291,8 @@
     source_in = jnp.zeros(col.shape, jnp.int32)
     for at, flip in enumerate(flips):
         source_in = jnp.where(part == at, inner ^ flip, source_in)
-    source_plane = plane ^ ((col % genes_dev) // each)
+    step = (col % genes_dev) // each
+    source_plane = plane ^ jnp.where(step == 0, 0, classes - step)
     source = source_plane * QUAD + source_in
     named = source * genes_dev + (col % each) * classes + plane
     pick = jnp.where(gene == named, 1.0, 0.0).astype(jnp.bfloat16)
@@ -321,7 +332,7 @@
 
 
 def score(member, share, parts):
-    rows, pairs = member.shape
+    rows, _ = member.shape
     _, sims = parts[0].shape
     return pl.pallas_call(
         score_kernel,
@@ -351,21 +362,23 @@
     lent = lending(block_count, classes, table, before, prefix)
     back = send(lent, perm=[(i + 1, i) for i in range(size - 1)])
     _, sums = closing(classes, table, own, lent, next_factor, next_normals, prefix)
-    paths, sums = lax.optimization_barrier((gene_pathways.T, sums))
-    rows = PATHWAYS // size
-    member, share = members(classes, (0, 2, 1, 3), genes, rows, paths)
-    back, member, share = lax.optimization_barrier((back, member, share))
     pieces = combine(classes, float(capacity), [sums, back])
 
-    flip = lambda x, bits: send(x, perm=[(i, i ^ bits) for i in range(size)])
-    arrived = [flip(pieces[apart], apart * QUAD) for apart in reversed(range(1, classes))]
-    arrived = [pieces[0]] + arrived[::-1]
-    mine = jnp.concatenate(arrived, axis=0)
-    across = flip(mine, 2)
-    partner = flip(mine, 1)
-    corner = flip(across, 1)
-
-    return score(member, share, [mine, across, partner, corner])
+    def flip(x, bits):
+        return send(x, perm=[(i, i ^ bits) for i in range(size)])
+
+    arrived = [pieces[0]]
+    for apart in reversed(range(1, classes)):
+        arrived.append(flip(pieces[apart], apart * QUAD))
+    half = classes // 2
+    early, late = jnp.concatenate(arrived[:half], axis=0), jnp.concatenate(arrived[half:], axis=0)
+    across_early = flip(early, 2)
+    across_late = flip(late, 2)
+    partner = flip(jnp.concatenate([early, late], axis=0), 1)
+    corner_early = flip(across_early, 1)
+    corner_late = flip(across_late, 1)
+    member, share = members(classes, (0, 2, 1, 3), genes, PATHWAYS // size, gene_pathways.T)
+    return score(member, share, [early, late, across_early, across_late, partner, corner_early, corner_late])
 
 
 def solution(mesh):

time: 34.4 us -> 33.7 us (0.980); the launches traced: 33.9 us -> 33.6 us
  waiting for transfers between devices: 10.2 us -> 8.87 us
  starting transfers between devices: 14 us -> 14.5 us
  Pallas kernels: 9.54 us -> 10 us
    ppermute x6 -> x8, waiting for transfers between devices: 10.1 us -> 8.87 us  [flip(): return send(x, perm=[(i, i ^ bits) for i in range(size)])]
    pallas_call x1, Pallas kernels: 3.78 us -> 4.49 us  [closing(): pl.pallas_call(functools.partial(closing_kernel, classes), out_shape=[jax...]
    ppermute x6 -> x8, starting transfers between devices: 10.3 us -> 10.8 us  [flip(): return send(x, perm=[(i, i ^ bits) for i in range(size)])]
  transfers between devices with their start and end apart: 8 -> 10, of which waited for: 5 -> 6; matrix products, arithmetic and copies ran while one was open for 0% -> 0% of each run, Pallas kernels for 21% -> 23%
where the time goes in v4:
time: 33.7 us; the launch traced here: 33.6 us
  starting transfers between devices  14.5 us (43%)
  Pallas kernels  10 us (30%)
  waiting for transfers between devices  8.87 us (26%)
    ppermute x8, starting transfers between devices, flip(): return send(x, perm=[(i, i ^ bits) for i in range(size)])  10.8 us
    ppermute x8, waiting for transfers between devices, flip(): return send(x, perm=[(i, i ^ bits) for i in range(size)])  8.87 us
    pallas_call x1, Pallas kernels, closing(): pl.pallas_call(functools.partial(closing_kernel, classes), out_shape=[jax...  4.49 us
    pallas_call x1, Pallas kernels, opening(): pl.pallas_call(opening_kernel, out_shape=[shape((sims // LANES, block_cou...  3.06 us
    ppermute x1, starting transfers between devices, local(): before = send(own, perm=[(i, i + 1) for i in range(size - 1)])  2.39 us
    ppermute x1, starting transfers between devices, local(): back = send(lent, perm=[(i + 1, i) for i in range(size - 1)])  1.29 us
    pallas_call x1, Pallas kernels, score(): pl.pallas_call(score_kernel, out_shape=jax.ShapeDtypeStruct((rows, sims),...  1.24 us
    pallas_call x1, Pallas kernels, lending(): pl.pallas_call(functools.partial(lending_kernel, block_count, classes), o...  0.89 us
  transfers between devices with their start and end apart: 10, of which 6 were waited for; matrix products, arithmetic and copies ran while one was open for 0% of the time, Pallas kernels for 23%

profile of v4, /device:TPU:0, one launch (start us, length us, event | category | flops | bytes accessed | tf_op | source)
XLA Modules:
  0.0 33.6 jit_solution(12559685214181320234)
XLA Ops:
  0.0 2.4 %collective-permute-start = (s32[2,64]{1,0:T(2,128)}, s32[2,64]{1,0:T(2,128)S(1)}, u32[]{:S(2)}, u32[]{:S(2)}) collective-permute-start(s32[2,64]{1,0:T(2,128)} %bitcast.3), channel_id=1, source_target_pairs={{0,1},{1,2},{2,3},{3,4},{4,5},{5,6},{6,7},{7,8},{8,9},{9,10},{10,1... | collective-permute-start | bytes 1544 | tf_op jit(solution)/shard_map/ppermute | solution.py:359
  2.4 3.1 %opening.1 = (f32[8,6168,128]{2,1,0:T(8,128)S(1)}, bf16[2,2048,256]{2,1,0:T(8,128)(2,1)S(1)}, bf16[2,256,1024]{2,1,0:T(8,128)(2,1)S(1)}, s32[8,128]{1,0:T(8,128)S(1)}) custom-call(s32[3]{0:T(128)} %lens.1, s32[3]{0:T(128)} %ranks.1, bf16[3,2048,256]{2,1,0:T(8,128)(2,1)} %factor.1, bf16[3,256,1024]{2,1,0:T(8,128)(2,1)} %normals.1), custom_call_target="tpu_custom_call" | custom-call | tf_op jit(solution)/shard_map/opening/pallas_call | solution.py:183
  5.5 0.0 collective-permute-done.spans
  5.5 0.0 copy-start.1
  5.5 0.9 %lending.1.lent = f32[64,1024]{1,0:T(8,128)S(1)} custom-call(s32[8,128]{1,0:T(8,128)S(1)} %get-tuple-element.18.table, s32[2,64]{1,0:T(2,128)S(1)} %collective-permute-done.spans, f32[8,6168,128]{2,1,0:T(8,128)S(1)} %get-tuple-element.19.prefix.old_prefix), custom_call_target="tpu_custom_call" | custom-call | tf_op jit(solution)/shard_map/lending/pallas_call | solution.py:209
  6.4 1.3 %collective-permute-start.1 = (f32[64,1024]{1,0:T(8,128)S(1)}, f32[64,1024]{1,0:T(8,128)S(1)}, u32[]{:S(2)}, u32[]{:S(2)}) collective-permute-start(f32[64,1024]{1,0:T(8,128)S(1)} %lending.1.lent), channel_id=1, source_target_pairs={{1,0},{2,1},{3,2},{4,3},{5,4},{6,5},{7,6},{8,7},{9,8},{10,9},{11,1... | collective-permute-start | bytes 786440 | tf_op jit(solution)/shard_map/ppermute | solution.py:363
  7.7 0.0 copy-start
  7.7 4.5 %closing.1 = (f32[8,6168,128]{2,1,0:T(8,128)S(1)}, f32[64,1024]{1,0:T(8,128)S(1)}) custom-call(s32[8,128]{1,0:T(8,128)S(1)} %get-tuple-element.18.table, s32[2,64]{1,0:T(2,128)S(1)} %bitcast.4, f32[64,1024]{1,0:T(8,128)S(1)} %lending.1.lent, bf16[2,2048,256]{2,1,0:T(8,128)(2,1)S(1)} %get-tuple-element.20.factor, ...), custom_call_target="tpu_custom_call", output_to_operand_aliasing={{0}: (5, {})} | custom-call | flops 3221225472 | bytes 16777216 | tf_op jit(solution)/shard_map/closing/pallas_call | solution.py:230
  12.2 0.1 combine.1
  12.3 8.0 %collective-permute-start.2 = (bf16[16,1024]{1,0:T(8,128)(2,1)S(1)}, bf16[16,1024]{1,0:T(8,128)(2,1)S(1)}, u32[]{:S(2)}, u32[]{:S(2)}) collective-permute-start(bf16[16,1024]{1,0:T(8,128)(2,1)S(1)} %get-tuple-element.24), channel_id=1, source_target_pairs={{0,12},{1,13},{2,14},{3,15},{4,8},{5,9},{6,10},{7,11},{8,4},{9,5},... | collective-permute-start | bytes 98312 | tf_op jit(solution)/shard_map/ppermute | solution.py:368
  20.2 0.0 collective-permute-start.3
  20.2 0.6 %collective-permute-start.4 = (bf16[16,1024]{1,0:T(8,128)(2,1)S(1)}, bf16[16,1024]{1,0:T(8,128)(2,1)S(1)}, u32[]{:S(2)}, u32[]{:S(2)}) collective-permute-start(bf16[16,1024]{1,0:T(8,128)(2,1)S(1)} %get-tuple-element.26), channel_id=1, source_target_pairs={{0,4},{1,5},{2,6},{3,7},{4,0},{5,1},{6,2},{7,3},{8,12},{9,13},{10,... | collective-permute-start | bytes 98312 | tf_op jit(solution)/shard_map/ppermute | solution.py:368
  20.9 1.2 %collective-permute-done.2 = bf16[16,1024]{1,0:T(8,128)(2,1)S(1)} collective-permute-done((bf16[16,1024]{1,0:T(8,128)(2,1)S(1)}, bf16[16,1024]{1,0:T(8,128)(2,1)S(1)}, u32[]{:S(2)}, u32[]{:S(2)}) %collective-permute-start.2) | collective-permute-done | bytes 32800 | tf_op jit(solution)/shard_map/ppermute | solution.py:368
  22.1 2.9 %collective-permute-done.3 = bf16[16,1024]{1,0:T(8,128)(2,1)S(1)} collective-permute-done((bf16[16,1024]{1,0:T(8,128)(2,1)S(1)}, bf16[16,1024]{1,0:T(8,128)(2,1)S(1)}, u32[]{:S(2)}, u32[]{:S(2)}) %collective-permute-start.3) | collective-permute-done | bytes 32800 | tf_op jit(solution)/shard_map/ppermute | solution.py:368
  25.1 0.0 collective-permute-done.4
  25.1 0.1 collective-permute-start.7
  25.2 0.1 collective-permute-start.6
  25.3 2.0 %collective-permute-start.5 = (bf16[32,1024]{1,0:T(8,128)(2,1)S(1)}, bf16[32,1024]{1,0:T(8,128)(2,1)S(1)}, u32[]{:S(2)}, u32[]{:S(2)}) collective-permute-start(bf16[32,1024]{1,0:T(8,128)(2,1)S(1)} %constant_dynamic-update-slice_fusion.refs_0_), channel_id=1, source_target_pairs={{0,2},{1,3},{2,0},{3,1},{4,6},{5,7},{6,4},{7,5},{8,10},{9,11},{10,... | collective-permute-start | bytes 196616 | tf_op jit(solution)/shard_map/ppermute | solution.py:368
  27.3 2.9 %collective-permute-done.6.refs_3_ = bf16[32,1024]{1,0:T(8,128)(2,1)S(1)} collective-permute-done((bf16[32,1024]{1,0:T(8,128)(2,1)S(1)}, bf16[32,1024]{1,0:T(8,128)(2,1)S(1)}, u32[]{:S(2)}, u32[]{:S(2)}) %collective-permute-start.6) | collective-permute-done | bytes 65568 | tf_op jit(solution)/shard_map/ppermute | solution.py:368
  30.2 0.8 %collective-permute-done.5.refs_2_ = bf16[32,1024]{1,0:T(8,128)(2,1)S(1)} collective-permute-done((bf16[32,1024]{1,0:T(8,128)(2,1)S(1)}, bf16[32,1024]{1,0:T(8,128)(2,1)S(1)}, u32[]{:S(2)}, u32[]{:S(2)}) %collective-permute-start.5) | collective-permute-done | bytes 65568 | tf_op jit(solution)/shard_map/ppermute | solution.py:368
  31.1 0.3 members.1
  31.4 0.1 collective-permute-done.9.refs_6_
  31.5 0.8 %collective-permute-done.8.refs_5_ = bf16[32,1024]{1,0:T(8,128)(2,1)S(1)} collective-permute-done((bf16[32,1024]{1,0:T(8,128)(2,1)S(1)}, bf16[32,1024]{1,0:T(8,128)(2,1)S(1)}, u32[]{:S(2)}, u32[]{:S(2)}) %collective-permute-start.8) | collective-permute-done | bytes 65568 | tf_op jit(solution)/shard_map/ppermute | solution.py:368
  32.3 1.2 %score.1 = f32[256,1024]{1,0:T(8,128)} custom-call(bf16[256,256]{1,0:T(8,128)(2,1)S(1)} %get-tuple-element.16.member, f32[256,1]{1,0:T(8,128)S(1)} %get-tuple-element.17.share, bf16[32,1024]{1,0:T(8,128)(2,1)S(1)} %constant_dynamic-update-slice_fusion.refs_0_, bf16[32,1024]{1,0:T(8,128)(2,1)S(1)} %constant_dynamic-update-slice_fusion.2.refs_1_, ...), custom_call_target="tpu_custom_call" | custom-call | tf_op jit(solution)/shard_map/score/pallas_call | solution.py:337
  (11 shorter events, 0.0 us)
Async XLA Ops:
  0.0 5.5 %collective-permute-start = (s32[2,64]{1,0:T(2,128)}, s32[2,64]{1,0:T(2,128)S(1)}, u32[]{:S(2)}, u32[]{:S(2)}) collective-permute-start(s32[2,64]{1,0:T(2,128)} %bitcast.3), channel_id=1, source_target_pairs={{0,1},{1,2},{2,3},{3,4},{4,5},{5,6},{6,7},{7,8},{8,9},{9,10},{10,1... | collective-permute-start | bytes 1544 | tf_op jit(solution)/shard_map/ppermute | solution.py:359
  5.5 2.2 %copy-start.1 = (s32[64,2]{0,1:T(2,128)S(1)}, s32[64,2]{0,1:T(2,128)}, u32[]{:S(2)}) copy-start(s32[64,2]{0,1:T(2,128)} %param.10) | copy-start | bytes 1540
  6.4 5.8 %collective-permute-start.1 = (f32[64,1024]{1,0:T(8,128)S(1)}, f32[64,1024]{1,0:T(8,128)S(1)}, u32[]{:S(2)}, u32[]{:S(2)}) collective-permute-start(f32[64,1024]{1,0:T(8,128)S(1)} %lending.1.lent), channel_id=1, source_target_pairs={{1,0},{2,1},{3,2},{4,3},{5,4},{6,5},{7,6},{8,7},{9,8},{10,9},{11,1... | collective-permute-start | bytes 786440 | tf_op jit(solution)/shard_map/ppermute | solution.py:363
  7.7 23.4 %copy-start = (s32[1024,4]{0,1:T(4,128)S(1)}, s32[1024,4]{0,1:T(4,128)}, u32[]{:S(2)}) copy-start(s32[1024,4]{0,1:T(4,128)} %param.11) | copy-start | bytes 49156
  12.3 9.9 %collective-permute-start.2 = (bf16[16,1024]{1,0:T(8,128)(2,1)S(1)}, bf16[16,1024]{1,0:T(8,128)(2,1)S(1)}, u32[]{:S(2)}, u32[]{:S(2)}) collective-permute-start(bf16[16,1024]{1,0:T(8,128)(2,1)S(1)} %get-tuple-element.24), channel_id=1, source_target_pairs={{0,12},{1,13},{2,14},{3,15},{4,8},{5,9},{6,10},{7,11},{8,4},{9,5},... | collective-permute-start | bytes 98312 | tf_op jit(solution)/shard_map/ppermute | solution.py:368
  20.2 4.8 %collective-permute-start.3 = (bf16[16,1024]{1,0:T(8,128)(2,1)S(1)}, bf16[16,1024]{1,0:T(8,128)(2,1)S(1)}, u32[]{:S(2)}, u32[]{:S(2)}) collective-permute-start(bf16[16,1024]{1,0:T(8,128)(2,1)S(1)} %get-tuple-element.25), channel_id=1, source_target_pairs={{0,8},{1,9},{2,10},{3,11},{4,12},{5,13},{6,14},{7,15},{8,0},{9,1},... | collective-permute-start | bytes 98312 | tf_op jit(solution)/shard_map/ppermute | solution.py:368
  20.2 4.8 %collective-permute-start.4 = (bf16[16,1024]{1,0:T(8,128)(2,1)S(1)}, bf16[16,1024]{1,0:T(8,128)(2,1)S(1)}, u32[]{:S(2)}, u32[]{:S(2)}) collective-permute-start(bf16[16,1024]{1,0:T(8,128)(2,1)S(1)} %get-tuple-element.26), channel_id=1, source_target_pairs={{0,4},{1,5},{2,6},{3,7},{4,0},{5,1},{6,2},{7,3},{8,12},{9,13},{10,... | collective-permute-start | bytes 98312 | tf_op jit(solution)/shard_map/ppermute | solution.py:368
  25.1 6.3 %collective-permute-start.7 = (bf16[64,1024]{1,0:T(8,128)(2,1)S(1)}, bf16[64,1024]{1,0:T(8,128)(2,1)S(1)}, u32[]{:S(2)}, u32[]{:S(2)}) collective-permute-start(bf16[64,1024]{1,0:T(8,128)(2,1)S(1)} %pad_maximum_fusion), channel_id=1, source_target_pairs={{0,1},{1,0},{2,3},{3,2},{4,5},{5,4},{6,7},{7,6},{8,9},{9,8},{10,11... | collective-permute-start | bytes 393224 | tf_op jit(solution)/shard_map/ppermute | solution.py:368
  25.2 5.0 %collective-permute-start.6 = (bf16[32,1024]{1,0:T(8,128)(2,1)S(1)}, bf16[32,1024]{1,0:T(8,128)(2,1)S(1)}, u32[]{:S(2)}, u32[]{:S(2)}) collective-permute-start(bf16[32,1024]{1,0:T(8,128)(2,1)S(1)} %constant_dynamic-update-slice_fusion.2.refs_1_), channel_id=1, source_target_pairs={{0,2},{1,3},{2,0},{3,1},{4,6},{5,7},{6,4},{7,5},{8,10},{9,11},{10,... | collective-permute-start | bytes 196616 | tf_op jit(solution)/shard_map/ppermute | solution.py:368
  25.3 5.8 %collective-permute-start.5 = (bf16[32,1024]{1,0:T(8,128)(2,1)S(1)}, bf16[32,1024]{1,0:T(8,128)(2,1)S(1)}, u32[]{:S(2)}, u32[]{:S(2)}) collective-permute-start(bf16[32,1024]{1,0:T(8,128)(2,1)S(1)} %constant_dynamic-update-slice_fusion.refs_0_), channel_id=1, source_target_pairs={{0,2},{1,3},{2,0},{3,1},{4,6},{5,7},{6,4},{7,5},{8,10},{9,11},{10,... | collective-permute-start | bytes 196616 | tf_op jit(solution)/shard_map/ppermute | solution.py:368
  30.2 1.3 %collective-permute-start.9 = (bf16[32,1024]{1,0:T(8,128)(2,1)S(1)}, bf16[32,1024]{1,0:T(8,128)(2,1)S(1)}, u32[]{:S(2)}, u32[]{:S(2)}) collective-permute-start(bf16[32,1024]{1,0:T(8,128)(2,1)S(1)} %collective-permute-done.6.refs_3_), channel_id=1, source_target_pairs={{0,1},{1,0},{2,3},{3,2},{4,5},{5,4},{6,7},{7,6},{8,9},{9,8},{10,11... | collective-permute-start | bytes 196616 | tf_op jit(solution)/shard_map/ppermute | solution.py:368
  31.1 1.3 %collective-permute-start.8 = (bf16[32,1024]{1,0:T(8,128)(2,1)S(1)}, bf16[32,1024]{1,0:T(8,128)(2,1)S(1)}, u32[]{:S(2)}, u32[]{:S(2)}) collective-permute-start(bf16[32,1024]{1,0:T(8,128)(2,1)S(1)} %collective-permute-done.5.refs_2_), channel_id=1, source_target_pairs={{0,1},{1,0},{2,3},{3,2},{4,5},{5,4},{6,7},{7,6},{8,9},{9,8},{10,11... | collective-permute-start | bytes 196616 | tf_op jit(solution)/shard_map/ppermute | solution.py:368

commit v5 on v4

--- a/solution.py
+++ b/solution.py
@@ -101,8 +101,9 @@
         copy.wait()
     genes = spans.shape[1]
     capacity = prefix.shape[1] // block_count - 8
-    base = lax.axis_index("genome") * block_count * capacity
-    length = table_in[block_count, 0]
+    device = lax.axis_index("genome")
+    base = device * block_count * capacity
+    length = jnp.where(device == 0, 0, table_in[block_count, 0])
     for first in range(0, genes, 8):
         side = first // 8 % parts.shape[0]
         ends = []
@@ -356,11 +357,11 @@
     send = functools.partial(lax.ppermute, axis_name="genome")
 
     own = gene_span.T
-    before = send(own, perm=[(i, i + 1) for i in range(size - 1)])
+    before = send(own, perm=[(i, (i + 1) % size) for i in range(size)])
     held = lambda x: pltpu.with_memory_space_constraint(x, pltpu.MemorySpace.HBM)
     prefix, next_factor, next_normals, table = opening(*map(held, (block_len, block_rank, factor, normals)))
     lent = lending(block_count, classes, table, before, prefix)
-    back = send(lent, perm=[(i + 1, i) for i in range(size - 1)])
+    back = send(lent, perm=[((i + 1) % size, i) for i in range(size)])
     _, sums = closing(classes, table, own, lent, next_factor, next_normals, prefix)
     pieces = combine(classes, float(capacity), [sums, back])
 

time: 33.7 us -> 29.9 us (0.89)
  starting transfers between devices: 14.5 us -> 8.84 us
  waiting for transfers between devices: 8.87 us -> 10.8 us
    ppermute x8, starting transfers between devices: 10.8 us -> 6.62 us  [flip(): return send(x, perm=[(i, i ^ bits) for i in range(size)])]
    ppermute x2, waiting for transfers between devices: 0.01 us -> 3.39 us  [the longest x1 3.38 us: local(): before = send(own, perm=[(i, (i + 1) % size) for i in range(size)])]
    ppermute x8, waiting for transfers between devices: 8.87 us -> 7.37 us  [flip(): return send(x, perm=[(i, i ^ bits) for i in range(size)])]
    ppermute x2, starting transfers between devices: 3.68 us -> 2.22 us  [the longest x1 1.73 us: local(): back = send(lent, perm=[((i + 1) % size, i) for i in range(size)])]
  transfers between devices with their start and end apart: 10 -> 10, of which waited for: 6 -> 7; matrix products, arithmetic and copies ran while one was open for 0% -> 0% of each run, Pallas kernels for 23% -> 26%
where the time goes in v5:
time: 29.9 us; the launch traced here: 29.8 us
  waiting for transfers between devices  10.8 us (36%)
  Pallas kernels  10 us (33%)
  starting transfers between devices  8.84 us (30%)
    ppermute x8, waiting for transfers between devices, flip(): return send(x, perm=[(i, i ^ bits) for i in range(size)])  7.37 us
    ppermute x8, starting transfers between devices, flip(): return send(x, perm=[(i, i ^ bits) for i in range(size)])  6.62 us
    pallas_call x1, Pallas kernels, closing(): pl.pallas_call(functools.partial(closing_kernel, classes), out_shape=[jax...  4.49 us
    ppermute x1, waiting for transfers between devices, local(): before = send(own, perm=[(i, (i + 1) % size) for i in range(size)])  3.38 us
    pallas_call x1, Pallas kernels, opening(): pl.pallas_call(opening_kernel, out_shape=[shape((sims // LANES, block_cou...  3.05 us
    ppermute x1, starting transfers between devices, local(): back = send(lent, perm=[((i + 1) % size, i) for i in range(size)])  1.73 us
    pallas_call x1, Pallas kernels, score(): pl.pallas_call(score_kernel, out_shape=jax.ShapeDtypeStruct((rows, sims),...  1.24 us
    pallas_call x1, Pallas kernels, lending(): pl.pallas_call(functools.partial(lending_kernel, block_count, classes), o...  0.89 us
  transfers between devices with their start and end apart: 10, of which 7 were waited for; matrix products, arithmetic and copies ran while one was open for 0% of the time, Pallas kernels for 26%

profile of v5, /device:TPU:0, one launch (start us, length us, event | category | flops | bytes accessed | tf_op | source)
XLA Modules:
  0.0 29.8 jit_solution(7296999504153045991)
XLA Ops:
  0.0 0.5 %collective-permute-start = (s32[2,64]{1,0:T(2,128)}, s32[2,64]{1,0:T(2,128)S(1)}, u32[]{:S(2)}, u32[]{:S(2)}) collective-permute-start(s32[2,64]{1,0:T(2,128)} %bitcast.3), channel_id=1, source_target_pairs={{0,1},{1,2},{2,3},{3,4},{4,5},{5,6},{6,7},{7,8},{8,9},{9,10},{10,1... | collective-permute-start | bytes 1544 | tf_op jit(solution)/shard_map/ppermute | solution.py:360
  0.5 3.1 %opening.1 = (f32[8,6168,128]{2,1,0:T(8,128)S(1)}, bf16[2,2048,256]{2,1,0:T(8,128)(2,1)S(1)}, bf16[2,256,1024]{2,1,0:T(8,128)(2,1)S(1)}, s32[8,128]{1,0:T(8,128)S(1)}) custom-call(s32[3]{0:T(128)} %lens.1, s32[3]{0:T(128)} %ranks.1, bf16[3,2048,256]{2,1,0:T(8,128)(2,1)} %factor.1, bf16[3,256,1024]{2,1,0:T(8,128)(2,1)} %normals.1), custom_call_target="tpu_custom_call" | custom-call | tf_op jit(solution)/shard_map/opening/pallas_call | solution.py:184
  3.6 3.4 %collective-permute-done.spans = s32[2,64]{1,0:T(2,128)S(1)} collective-permute-done((s32[2,64]{1,0:T(2,128)}, s32[2,64]{1,0:T(2,128)S(1)}, u32[]{:S(2)}, u32[]{:S(2)}) %collective-permute-start) | collective-permute-done | bytes 544 | tf_op jit(solution)/shard_map/ppermute | solution.py:360
  6.9 0.9 %lending.1.lent = f32[64,1024]{1,0:T(8,128)S(1)} custom-call(s32[8,128]{1,0:T(8,128)S(1)} %get-tuple-element.18.table, s32[2,64]{1,0:T(2,128)S(1)} %collective-permute-done.spans, f32[8,6168,128]{2,1,0:T(8,128)S(1)} %get-tuple-element.19.prefix.old_prefix), custom_call_target="tpu_custom_call" | custom-call | tf_op jit(solution)/shard_map/lending/pallas_call | solution.py:210
  7.8 1.7 %collective-permute-start.1 = (f32[64,1024]{1,0:T(8,128)S(1)}, f32[64,1024]{1,0:T(8,128)S(1)}, u32[]{:S(2)}, u32[]{:S(2)}) collective-permute-start(f32[64,1024]{1,0:T(8,128)S(1)} %lending.1.lent), channel_id=1, source_target_pairs={{1,0},{2,1},{3,2},{4,3},{5,4},{6,5},{7,6},{8,7},{9,8},{10,9},{11,1... | collective-permute-start | bytes 786440 | tf_op jit(solution)/shard_map/ppermute | solution.py:364
  9.6 4.5 %closing.1 = (f32[8,6168,128]{2,1,0:T(8,128)S(1)}, f32[64,1024]{1,0:T(8,128)S(1)}) custom-call(s32[8,128]{1,0:T(8,128)S(1)} %get-tuple-element.18.table, s32[2,64]{1,0:T(2,128)S(1)} %bitcast.4, f32[64,1024]{1,0:T(8,128)S(1)} %lending.1.lent, bf16[2,2048,256]{2,1,0:T(8,128)(2,1)S(1)} %get-tuple-element.20.factor, ...), custom_call_target="tpu_custom_call", output_to_operand_aliasing={{0}: (5, {})} | custom-call | flops 3221225472 | bytes 16777216 | tf_op jit(solution)/shard_map/closing/pallas_call | solution.py:231
  14.1 0.0 collective-permute-done.1.back
  14.1 0.1 combine.1
  14.1 2.3 %collective-permute-start.2 = (bf16[16,1024]{1,0:T(8,128)(2,1)S(1)}, bf16[16,1024]{1,0:T(8,128)(2,1)S(1)}, u32[]{:S(2)}, u32[]{:S(2)}) collective-permute-start(bf16[16,1024]{1,0:T(8,128)(2,1)S(1)} %get-tuple-element.24), channel_id=1, source_target_pairs={{0,12},{1,13},{2,14},{3,15},{4,8},{5,9},{6,10},{7,11},{8,4},{9,5},... | collective-permute-start | bytes 98312 | tf_op jit(solution)/shard_map/ppermute | solution.py:369
  16.5 2.1 %collective-permute-start.4 = (bf16[16,1024]{1,0:T(8,128)(2,1)S(1)}, bf16[16,1024]{1,0:T(8,128)(2,1)S(1)}, u32[]{:S(2)}, u32[]{:S(2)}) collective-permute-start(bf16[16,1024]{1,0:T(8,128)(2,1)S(1)} %get-tuple-element.26), channel_id=1, source_target_pairs={{0,4},{1,5},{2,6},{3,7},{4,0},{5,1},{6,2},{7,3},{8,12},{9,13},{10,... | collective-permute-start | bytes 98312 | tf_op jit(solution)/shard_map/ppermute | solution.py:369
  18.6 1.3 %collective-permute-done.2 = bf16[16,1024]{1,0:T(8,128)(2,1)S(1)} collective-permute-done((bf16[16,1024]{1,0:T(8,128)(2,1)S(1)}, bf16[16,1024]{1,0:T(8,128)(2,1)S(1)}, u32[]{:S(2)}, u32[]{:S(2)}) %collective-permute-start.2) | collective-permute-done | bytes 32800 | tf_op jit(solution)/shard_map/ppermute | solution.py:369
  19.9 1.3 %collective-permute-done.3 = bf16[16,1024]{1,0:T(8,128)(2,1)S(1)} collective-permute-done((bf16[16,1024]{1,0:T(8,128)(2,1)S(1)}, bf16[16,1024]{1,0:T(8,128)(2,1)S(1)}, u32[]{:S(2)}, u32[]{:S(2)}) %collective-permute-start.3) | collective-permute-done | bytes 32800 | tf_op jit(solution)/shard_map/ppermute | solution.py:369
  21.3 0.0 collective-permute-done.4
  21.3 0.1 collective-permute-start.7
  21.4 1.2 %collective-permute-start.6 = (bf16[32,1024]{1,0:T(8,128)(2,1)S(1)}, bf16[32,1024]{1,0:T(8,128)(2,1)S(1)}, u32[]{:S(2)}, u32[]{:S(2)}) collective-permute-start(bf16[32,1024]{1,0:T(8,128)(2,1)S(1)} %constant_dynamic-update-slice_fusion.2.refs_1_), channel_id=1, source_target_pairs={{0,2},{1,3},{2,0},{3,1},{4,6},{5,7},{6,4},{7,5},{8,10},{9,11},{10,... | collective-permute-start | bytes 196616 | tf_op jit(solution)/shard_map/ppermute | solution.py:369
  22.6 0.9 %collective-permute-start.5 = (bf16[32,1024]{1,0:T(8,128)(2,1)S(1)}, bf16[32,1024]{1,0:T(8,128)(2,1)S(1)}, u32[]{:S(2)}, u32[]{:S(2)}) collective-permute-start(bf16[32,1024]{1,0:T(8,128)(2,1)S(1)} %constant_dynamic-update-slice_fusion.refs_0_), channel_id=1, source_target_pairs={{0,2},{1,3},{2,0},{3,1},{4,6},{5,7},{6,4},{7,5},{8,10},{9,11},{10,... | collective-permute-start | bytes 196616 | tf_op jit(solution)/shard_map/ppermute | solution.py:369
  23.5 2.9 %collective-permute-done.6.refs_3_ = bf16[32,1024]{1,0:T(8,128)(2,1)S(1)} collective-permute-done((bf16[32,1024]{1,0:T(8,128)(2,1)S(1)}, bf16[32,1024]{1,0:T(8,128)(2,1)S(1)}, u32[]{:S(2)}, u32[]{:S(2)}) %collective-permute-start.6) | collective-permute-done | bytes 65568 | tf_op jit(solution)/shard_map/ppermute | solution.py:369
  26.4 0.0 collective-permute-start.9
  26.4 0.8 %collective-permute-done.5.refs_2_ = bf16[32,1024]{1,0:T(8,128)(2,1)S(1)} collective-permute-done((bf16[32,1024]{1,0:T(8,128)(2,1)S(1)}, bf16[32,1024]{1,0:T(8,128)(2,1)S(1)}, u32[]{:S(2)}, u32[]{:S(2)}) %collective-permute-start.5) | collective-permute-done | bytes 65568 | tf_op jit(solution)/shard_map/ppermute | solution.py:369
  27.3 0.0 collective-permute-start.8
  27.3 0.3 %members.1 = (bf16[256,256]{1,0:T(8,128)(2,1)S(1)}, f32[256,1]{1,0:T(8,128)S(1)}) custom-call(s32[4,1024]{1,0:T(4,128)S(1)} %bitcast.2), custom_call_target="tpu_custom_call" | custom-call | tf_op jit(solution)/shard_map/members/pallas_call | solution.py:309
  27.6 0.1 collective-permute-done.9.refs_6_
  27.7 0.8 %collective-permute-done.8.refs_5_ = bf16[32,1024]{1,0:T(8,128)(2,1)S(1)} collective-permute-done((bf16[32,1024]{1,0:T(8,128)(2,1)S(1)}, bf16[32,1024]{1,0:T(8,128)(2,1)S(1)}, u32[]{:S(2)}, u32[]{:S(2)}) %collective-permute-start.8) | collective-permute-done | bytes 65568 | tf_op jit(solution)/shard_map/ppermute | solution.py:369
  28.5 1.2 %score.1 = f32[256,1024]{1,0:T(8,128)} custom-call(bf16[256,256]{1,0:T(8,128)(2,1)S(1)} %get-tuple-element.16.member, f32[256,1]{1,0:T(8,128)S(1)} %get-tuple-element.17.share, bf16[32,1024]{1,0:T(8,128)(2,1)S(1)} %constant_dynamic-update-slice_fusion.refs_0_, bf16[32,1024]{1,0:T(8,128)(2,1)S(1)} %constant_dynamic-update-slice_fusion.2.refs_1_, ...), custom_call_target="tpu_custom_call" | custom-call | tf_op jit(solution)/shard_map/score/pallas_call | solution.py:338
  (11 shorter events, 0.0 us)
Async XLA Ops:
  0.0 6.9 %collective-permute-start = (s32[2,64]{1,0:T(2,128)}, s32[2,64]{1,0:T(2,128)S(1)}, u32[]{:S(2)}, u32[]{:S(2)}) collective-permute-start(s32[2,64]{1,0:T(2,128)} %bitcast.3), channel_id=1, source_target_pairs={{0,1},{1,2},{2,3},{3,4},{4,5},{5,6},{6,7},{7,8},{8,9},{9,10},{10,1... | collective-permute-start | bytes 1544 | tf_op jit(solution)/shard_map/ppermute | solution.py:360
  6.9 2.6 %copy-start.1 = (s32[64,2]{0,1:T(2,128)S(1)}, s32[64,2]{0,1:T(2,128)}, u32[]{:S(2)}) copy-start(s32[64,2]{0,1:T(2,128)} %param.10) | copy-start | bytes 1540
  7.8 6.2 %collective-permute-start.1 = (f32[64,1024]{1,0:T(8,128)S(1)}, f32[64,1024]{1,0:T(8,128)S(1)}, u32[]{:S(2)}, u32[]{:S(2)}) collective-permute-start(f32[64,1024]{1,0:T(8,128)S(1)} %lending.1.lent), channel_id=1, source_target_pairs={{1,0},{2,1},{3,2},{4,3},{5,4},{6,5},{7,6},{8,7},{9,8},{10,9},{11,1... | collective-permute-start | bytes 786440 | tf_op jit(solution)/shard_map/ppermute | solution.py:364
  9.6 17.7 %copy-start = (s32[1024,4]{0,1:T(4,128)S(1)}, s32[1024,4]{0,1:T(4,128)}, u32[]{:S(2)}) copy-start(s32[1024,4]{0,1:T(4,128)} %param.11) | copy-start | bytes 49156
  14.1 5.8 %collective-permute-start.2 = (bf16[16,1024]{1,0:T(8,128)(2,1)S(1)}, bf16[16,1024]{1,0:T(8,128)(2,1)S(1)}, u32[]{:S(2)}, u32[]{:S(2)}) collective-permute-start(bf16[16,1024]{1,0:T(8,128)(2,1)S(1)} %get-tuple-element.24), channel_id=1, source_target_pairs={{0,12},{1,13},{2,14},{3,15},{4,8},{5,9},{6,10},{7,11},{8,4},{9,5},... | collective-permute-start | bytes 98312 | tf_op jit(solution)/shard_map/ppermute | solution.py:369
  16.5 4.8 %collective-permute-start.3 = (bf16[16,1024]{1,0:T(8,128)(2,1)S(1)}, bf16[16,1024]{1,0:T(8,128)(2,1)S(1)}, u32[]{:S(2)}, u32[]{:S(2)}) collective-permute-start(bf16[16,1024]{1,0:T(8,128)(2,1)S(1)} %get-tuple-element.25), channel_id=1, source_target_pairs={{0,8},{1,9},{2,10},{3,11},{4,12},{5,13},{6,14},{7,15},{8,0},{9,1},... | collective-permute-start | bytes 98312 | tf_op jit(solution)/shard_map/ppermute | solution.py:369
  16.5 4.8 %collective-permute-start.4 = (bf16[16,1024]{1,0:T(8,128)(2,1)S(1)}, bf16[16,1024]{1,0:T(8,128)(2,1)S(1)}, u32[]{:S(2)}, u32[]{:S(2)}) collective-permute-start(bf16[16,1024]{1,0:T(8,128)(2,1)S(1)} %get-tuple-element.26), channel_id=1, source_target_pairs={{0,4},{1,5},{2,6},{3,7},{4,0},{5,1},{6,2},{7,3},{8,12},{9,13},{10,... | collective-permute-start | bytes 98312 | tf_op jit(solution)/shard_map/ppermute | solution.py:369
  21.3 6.3 %collective-permute-start.7 = (bf16[64,1024]{1,0:T(8,128)(2,1)S(1)}, bf16[64,1024]{1,0:T(8,128)(2,1)S(1)}, u32[]{:S(2)}, u32[]{:S(2)}) collective-permute-start(bf16[64,1024]{1,0:T(8,128)(2,1)S(1)} %pad_maximum_fusion), channel_id=1, source_target_pairs={{0,1},{1,0},{2,3},{3,2},{4,5},{5,4},{6,7},{7,6},{8,9},{9,8},{10,11... | collective-permute-start | bytes 393224 | tf_op jit(solution)/shard_map/ppermute | solution.py:369
  21.4 5.0 %collective-permute-start.6 = (bf16[32,1024]{1,0:T(8,128)(2,1)S(1)}, bf16[32,1024]{1,0:T(8,128)(2,1)S(1)}, u32[]{:S(2)}, u32[]{:S(2)}) collective-permute-start(bf16[32,1024]{1,0:T(8,128)(2,1)S(1)} %constant_dynamic-update-slice_fusion.2.refs_1_), channel_id=1, source_target_pairs={{0,2},{1,3},{2,0},{3,1},{4,6},{5,7},{6,4},{7,5},{8,10},{9,11},{10,... | collective-permute-start | bytes 196616 | tf_op jit(solution)/shard_map/ppermute | solution.py:369
  22.6 4.6 %collective-permute-start.5 = (bf16[32,1024]{1,0:T(8,128)(2,1)S(1)}, bf16[32,1024]{1,0:T(8,128)(2,1)S(1)}, u32[]{:S(2)}, u32[]{:S(2)}) collective-permute-start(bf16[32,1024]{1,0:T(8,128)(2,1)S(1)} %constant_dynamic-update-slice_fusion.refs_0_), channel_id=1, source_target_pairs={{0,2},{1,3},{2,0},{3,1},{4,6},{5,7},{6,4},{7,5},{8,10},{9,11},{10,... | collective-permute-start | bytes 196616 | tf_op jit(solution)/shard_map/ppermute | solution.py:369
  26.4 1.3 %collective-permute-start.9 = (bf16[32,1024]{1,0:T(8,128)(2,1)S(1)}, bf16[32,1024]{1,0:T(8,128)(2,1)S(1)}, u32[]{:S(2)}, u32[]{:S(2)}) collective-permute-start(bf16[32,1024]{1,0:T(8,128)(2,1)S(1)} %collective-permute-done.6.refs_3_), channel_id=1, source_target_pairs={{0,1},{1,0},{2,3},{3,2},{4,5},{5,4},{6,7},{7,6},{8,9},{9,8},{10,11... | collective-permute-start | bytes 196616 | tf_op jit(solution)/shard_map/ppermute | solution.py:369
  27.3 1.3 %collective-permute-start.8 = (bf16[32,1024]{1,0:T(8,128)(2,1)S(1)}, bf16[32,1024]{1,0:T(8,128)(2,1)S(1)}, u32[]{:S(2)}, u32[]{:S(2)}) collective-permute-start(bf16[32,1024]{1,0:T(8,128)(2,1)S(1)} %collective-permute-done.5.refs_2_), channel_id=1, source_target_pairs={{0,1},{1,0},{2,3},{3,2},{4,5},{5,4},{6,7},{7,6},{8,9},{9,8},{10,11... | collective-permute-start | bytes 196616 | tf_op jit(solution)/shard_map/ppermute | solution.py:369

commit v6 on v5

--- a/solution.py
+++ b/solution.py
@@ -10,10 +10,14 @@
 
 PATHWAYS = 4096
 QUAD = 4
-CHUNK = 1024
+CHUNK = 2048
 COLS = 256
 LANES = 128
 VMEM = pltpu.MemorySpace.VMEM
+
+
+def order_of(classes):
+    return list(range(classes // 2, classes)) + list(range(classes // 2 - 1, 0, -1))
 
 
 def reduce_parts(parts, side, out, first):
@@ -102,24 +106,25 @@
     genes = spans.shape[1]
     capacity = prefix.shape[1] // block_count - 8
     device = lax.axis_index("genome")
-    base = device * block_count * capacity
-    length = jnp.where(device == 0, 0, table_in[block_count, 0])
+    base = jnp.where(device == 0, 1 << 30, device * block_count * capacity)
+    length = table_in[block_count, 0]
     for first in range(0, genes, 8):
         side = first // 8 % parts.shape[0]
         ends = []
         for slot in range(8):
             gene = class_major(first + slot, genes // classes, classes)
-            ends.append(jnp.clip(spans_in[1, gene] - base, 0, length))
+            ends.append(spans_in[1, gene])
         reach = functools.reduce(jnp.maximum, ends)
 
-        @pl.when(reach > 0)
+        @pl.when(reach > base)
         def _():
             for slot, end in enumerate(ends):
+                end = jnp.clip(end - base, 0, length)
                 for tile in range(prefix.shape[0]):
                     parts[side, tile, slot * 8:slot * 8 + 8, :] = prefix[tile, pl.ds(end, 8), :]
             reduce_parts(parts, side, out, first)
 
-        @pl.when(reach == 0)
+        @pl.when(reach <= base)
         def _():
             out[first:first + 8, :] = jnp.zeros((8, out.shape[1]), jnp.float32)
 
@@ -293,7 +298,10 @@
     for at, flip in enumerate(flips):
         source_in = jnp.where(part == at, inner ^ flip, source_in)
     step = (col % genes_dev) // each
-    source_plane = plane ^ jnp.where(step == 0, 0, classes - step)
+    apart = jnp.zeros(col.shape, jnp.int32)
+    for at, planes in enumerate(order_of(classes)):
+        apart = jnp.where(step == at + 1, planes, apart)
+    source_plane = plane ^ apart
     source = source_plane * QUAD + source_in
     named = source * genes_dev + (col % each) * classes + plane
     pick = jnp.where(gene == named, 1.0, 0.0).astype(jnp.bfloat16)
@@ -369,7 +377,7 @@
         return send(x, perm=[(i, i ^ bits) for i in range(size)])
 
     arrived = [pieces[0]]
-    for apart in reversed(range(1, classes)):
+    for apart in order_of(classes):
         arrived.append(flip(pieces[apart], apart * QUAD))
     half = classes // 2
     early, late = jnp.concatenate(arrived[:half], axis=0), jnp.concatenate(arrived[half:], axis=0)

time: 29.9 us -> 29.5 us (0.987)
  starting transfers between devices: 8.84 us -> 7.94 us
  waiting for transfers between devices: 10.8 us -> 11.7 us
  Pallas kernels: 10 us -> 9.61 us
    ppermute x8, waiting for transfers between devices: 7.37 us -> 8.31 us  [flip(): return send(x, perm=[(i, i ^ bits) for i in range(size)])]
    ppermute x8, starting transfers between devices: 6.62 us -> 5.72 us  [flip(): return send(x, perm=[(i, i ^ bits) for i in range(size)])]
    pallas_call x1, Pallas kernels: 4.49 us -> 4.15 us  [closing(): pl.pallas_call(functools.partial(closing_kernel, classes), out_shape=[jax...]
where the time goes in v6:
time: 29.5 us; the launch traced here: 29.4 us
  waiting for transfers between devices  11.7 us (40%)
  Pallas kernels  9.61 us (33%)
  starting transfers between devices  7.94 us (27%)
    ppermute x8, waiting for transfers between devices, flip(): return send(x, perm=[(i, i ^ bits) for i in range(size)])  8.31 us
    ppermute x8, starting transfers between devices, flip(): return send(x, perm=[(i, i ^ bits) for i in range(size)])  5.72 us
    pallas_call x1, Pallas kernels, closing(): pl.pallas_call(functools.partial(closing_kernel, classes), out_shape=[jax...  4.15 us
    ppermute x1, waiting for transfers between devices, local(): before = send(own, perm=[(i, (i + 1) % size) for i in range(size)])  3.39 us
    pallas_call x1, Pallas kernels, opening(): pl.pallas_call(opening_kernel, out_shape=[shape((sims // LANES, block_cou...  3.05 us
    ppermute x1, starting transfers between devices, local(): back = send(lent, perm=[((i + 1) % size, i) for i in range(size)])  1.73 us
    pallas_call x1, Pallas kernels, score(): pl.pallas_call(score_kernel, out_shape=jax.ShapeDtypeStruct((rows, sims),...  1.24 us
    pallas_call x1, Pallas kernels, lending(): pl.pallas_call(functools.partial(lending_kernel, block_count, classes), o...  0.81 us
  transfers between devices with their start and end apart: 10, of which 7 were waited for; matrix products, arithmetic and copies ran while one was open for 0% of the time, Pallas kernels for 26%

profile of v6, /device:TPU:0, one launch (start us, length us, event | category | flops | bytes accessed | tf_op | source)
XLA Modules:
  0.0 29.4 jit_solution(9245751250495182196)
XLA Ops:
  0.0 0.5 %collective-permute-start = (s32[2,64]{1,0:T(2,128)}, s32[2,64]{1,0:T(2,128)S(1)}, u32[]{:S(2)}, u32[]{:S(2)}) collective-permute-start(s32[2,64]{1,0:T(2,128)} %bitcast.3), channel_id=1, source_target_pairs={{0,1},{1,2},{2,3},{3,4},{4,5},{5,6},{6,7},{7,8},{8,9},{9,10},{10,1... | collective-permute-start | bytes 1544 | tf_op jit(solution)/shard_map/ppermute | solution.py:368
  0.5 3.0 %opening.1 = (f32[8,6168,128]{2,1,0:T(8,128)S(1)}, bf16[2,2048,256]{2,1,0:T(8,128)(2,1)S(1)}, bf16[2,256,1024]{2,1,0:T(8,128)(2,1)S(1)}, s32[8,128]{1,0:T(8,128)S(1)}) custom-call(s32[3]{0:T(128)} %lens.1, s32[3]{0:T(128)} %ranks.1, bf16[3,2048,256]{2,1,0:T(8,128)(2,1)} %factor.1, bf16[3,256,1024]{2,1,0:T(8,128)(2,1)} %normals.1), custom_call_target="tpu_custom_call" | custom-call | tf_op jit(solution)/shard_map/opening/pallas_call | solution.py:189
  3.5 3.4 %collective-permute-done.spans = s32[2,64]{1,0:T(2,128)S(1)} collective-permute-done((s32[2,64]{1,0:T(2,128)}, s32[2,64]{1,0:T(2,128)S(1)}, u32[]{:S(2)}, u32[]{:S(2)}) %collective-permute-start) | collective-permute-done | bytes 544 | tf_op jit(solution)/shard_map/ppermute | solution.py:368
  6.9 0.8 %lending.1.lent = f32[64,1024]{1,0:T(8,128)S(1)} custom-call(s32[8,128]{1,0:T(8,128)S(1)} %get-tuple-element.18.table, s32[2,64]{1,0:T(2,128)S(1)} %collective-permute-done.spans, f32[8,6168,128]{2,1,0:T(8,128)S(1)} %get-tuple-element.19.prefix.old_prefix), custom_call_target="tpu_custom_call" | custom-call | tf_op jit(solution)/shard_map/lending/pallas_call | solution.py:215
  7.8 1.7 %collective-permute-start.1 = (f32[64,1024]{1,0:T(8,128)S(1)}, f32[64,1024]{1,0:T(8,128)S(1)}, u32[]{:S(2)}, u32[]{:S(2)}) collective-permute-start(f32[64,1024]{1,0:T(8,128)S(1)} %lending.1.lent), channel_id=1, source_target_pairs={{1,0},{2,1},{3,2},{4,3},{5,4},{6,5},{7,6},{8,7},{9,8},{10,9},{11,1... | collective-permute-start | bytes 786440 | tf_op jit(solution)/shard_map/ppermute | solution.py:372
  9.5 4.1 %closing.1 = (f32[8,6168,128]{2,1,0:T(8,128)S(1)}, f32[64,1024]{1,0:T(8,128)S(1)}) custom-call(s32[8,128]{1,0:T(8,128)S(1)} %get-tuple-element.18.table, s32[2,64]{1,0:T(2,128)S(1)} %bitcast.4, f32[64,1024]{1,0:T(8,128)S(1)} %lending.1.lent, bf16[2,2048,256]{2,1,0:T(8,128)(2,1)S(1)} %get-tuple-element.20.factor, ...), custom_call_target="tpu_custom_call", output_to_operand_aliasing={{0}: (5, {})} | custom-call | flops 3221225472 | bytes 16777216 | tf_op jit(solution)/shard_map/closing/pallas_call | solution.py:236
  13.7 0.0 collective-permute-done.1.back
  13.7 0.1 combine.1
  13.7 1.3 %collective-permute-start.2 = (bf16[16,1024]{1,0:T(8,128)(2,1)S(1)}, bf16[16,1024]{1,0:T(8,128)(2,1)S(1)}, u32[]{:S(2)}, u32[]{:S(2)}) collective-permute-start(bf16[16,1024]{1,0:T(8,128)(2,1)S(1)} %get-tuple-element.24), channel_id=1, source_target_pairs={{0,8},{1,9},{2,10},{3,11},{4,12},{5,13},{6,14},{7,15},{8,0},{9,1},... | collective-permute-start | bytes 98312 | tf_op jit(solution)/shard_map/ppermute | solution.py:377
  15.0 1.3 %collective-permute-start.3 = (bf16[16,1024]{1,0:T(8,128)(2,1)S(1)}, bf16[16,1024]{1,0:T(8,128)(2,1)S(1)}, u32[]{:S(2)}, u32[]{:S(2)}) collective-permute-start(bf16[16,1024]{1,0:T(8,128)(2,1)S(1)} %get-tuple-element.25), channel_id=1, source_target_pairs={{0,12},{1,13},{2,14},{3,15},{4,8},{5,9},{6,10},{7,11},{8,4},{9,5},... | collective-permute-start | bytes 98312 | tf_op jit(solution)/shard_map/ppermute | solution.py:377
  16.4 0.9 %collective-permute-start.4 = (bf16[16,1024]{1,0:T(8,128)(2,1)S(1)}, bf16[16,1024]{1,0:T(8,128)(2,1)S(1)}, u32[]{:S(2)}, u32[]{:S(2)}) collective-permute-start(bf16[16,1024]{1,0:T(8,128)(2,1)S(1)} %get-tuple-element.26), channel_id=1, source_target_pairs={{0,4},{1,5},{2,6},{3,7},{4,0},{5,1},{6,2},{7,3},{8,12},{9,13},{10,... | collective-permute-start | bytes 98312 | tf_op jit(solution)/shard_map/ppermute | solution.py:377
  17.3 1.3 %collective-permute-done.2 = bf16[16,1024]{1,0:T(8,128)(2,1)S(1)} collective-permute-done((bf16[16,1024]{1,0:T(8,128)(2,1)S(1)}, bf16[16,1024]{1,0:T(8,128)(2,1)S(1)}, u32[]{:S(2)}, u32[]{:S(2)}) %collective-permute-start.2) | collective-permute-done | bytes 32800 | tf_op jit(solution)/shard_map/ppermute | solution.py:377
  18.6 2.2 %collective-permute-done.3 = bf16[16,1024]{1,0:T(8,128)(2,1)S(1)} collective-permute-done((bf16[16,1024]{1,0:T(8,128)(2,1)S(1)}, bf16[16,1024]{1,0:T(8,128)(2,1)S(1)}, u32[]{:S(2)}, u32[]{:S(2)}) %collective-permute-start.3) | collective-permute-done | bytes 32800 | tf_op jit(solution)/shard_map/ppermute | solution.py:377
  20.8 0.0 collective-permute-done.4
  20.9 0.1 collective-permute-start.7
  21.0 1.4 %collective-permute-start.6 = (bf16[32,1024]{1,0:T(8,128)(2,1)S(1)}, bf16[32,1024]{1,0:T(8,128)(2,1)S(1)}, u32[]{:S(2)}, u32[]{:S(2)}) collective-permute-start(bf16[32,1024]{1,0:T(8,128)(2,1)S(1)} %constant_dynamic-update-slice_fusion.2.refs_1_), channel_id=1, source_target_pairs={{0,2},{1,3},{2,0},{3,1},{4,6},{5,7},{6,4},{7,5},{8,10},{9,11},{10,... | collective-permute-start | bytes 196616 | tf_op jit(solution)/shard_map/ppermute | solution.py:377
  22.4 0.7 %collective-permute-start.5 = (bf16[32,1024]{1,0:T(8,128)(2,1)S(1)}, bf16[32,1024]{1,0:T(8,128)(2,1)S(1)}, u32[]{:S(2)}, u32[]{:S(2)}) collective-permute-start(bf16[32,1024]{1,0:T(8,128)(2,1)S(1)} %constant_dynamic-update-slice_fusion.refs_0_), channel_id=1, source_target_pairs={{0,2},{1,3},{2,0},{3,1},{4,6},{5,7},{6,4},{7,5},{8,10},{9,11},{10,... | collective-permute-start | bytes 196616 | tf_op jit(solution)/shard_map/ppermute | solution.py:377
  23.1 2.9 %collective-permute-done.6.refs_3_ = bf16[32,1024]{1,0:T(8,128)(2,1)S(1)} collective-permute-done((bf16[32,1024]{1,0:T(8,128)(2,1)S(1)}, bf16[32,1024]{1,0:T(8,128)(2,1)S(1)}, u32[]{:S(2)}, u32[]{:S(2)}) %collective-permute-start.6) | collective-permute-done | bytes 65568 | tf_op jit(solution)/shard_map/ppermute | solution.py:377
  26.0 0.0 collective-permute-start.9
  26.0 0.8 %collective-permute-done.5.refs_2_ = bf16[32,1024]{1,0:T(8,128)(2,1)S(1)} collective-permute-done((bf16[32,1024]{1,0:T(8,128)(2,1)S(1)}, bf16[32,1024]{1,0:T(8,128)(2,1)S(1)}, u32[]{:S(2)}, u32[]{:S(2)}) %collective-permute-start.5) | collective-permute-done | bytes 65568 | tf_op jit(solution)/shard_map/ppermute | solution.py:377
  26.9 0.3 %members.1 = (bf16[256,256]{1,0:T(8,128)(2,1)S(1)}, f32[256,1]{1,0:T(8,128)S(1)}) custom-call(s32[4,1024]{1,0:T(4,128)S(1)} %bitcast.2), custom_call_target="tpu_custom_call" | custom-call | tf_op jit(solution)/shard_map/members/pallas_call | solution.py:317
  27.2 0.1 collective-permute-done.9.refs_6_
  27.3 0.8 %collective-permute-done.8.refs_5_ = bf16[32,1024]{1,0:T(8,128)(2,1)S(1)} collective-permute-done((bf16[32,1024]{1,0:T(8,128)(2,1)S(1)}, bf16[32,1024]{1,0:T(8,128)(2,1)S(1)}, u32[]{:S(2)}, u32[]{:S(2)}) %collective-permute-start.8) | collective-permute-done | bytes 65568 | tf_op jit(solution)/shard_map/ppermute | solution.py:377
  28.2 1.2 %score.1 = f32[256,1024]{1,0:T(8,128)} custom-call(bf16[256,256]{1,0:T(8,128)(2,1)S(1)} %get-tuple-element.16.member, f32[256,1]{1,0:T(8,128)S(1)} %get-tuple-element.17.share, bf16[32,1024]{1,0:T(8,128)(2,1)S(1)} %constant_dynamic-update-slice_fusion.refs_0_, bf16[32,1024]{1,0:T(8,128)(2,1)S(1)} %constant_dynamic-update-slice_fusion.2.refs_1_, ...), custom_call_target="tpu_custom_call" | custom-call | tf_op jit(solution)/shard_map/score/pallas_call | solution.py:346
  (11 shorter events, 0.0 us)
Async XLA Ops:
  0.0 6.9 %collective-permute-start = (s32[2,64]{1,0:T(2,128)}, s32[2,64]{1,0:T(2,128)S(1)}, u32[]{:S(2)}, u32[]{:S(2)}) collective-permute-start(s32[2,64]{1,0:T(2,128)} %bitcast.3), channel_id=1, source_target_pairs={{0,1},{1,2},{2,3},{3,4},{4,5},{5,6},{6,7},{7,8},{8,9},{9,10},{10,1... | collective-permute-start | bytes 1544 | tf_op jit(solution)/shard_map/ppermute | solution.py:368
  6.9 2.6 %copy-start.1 = (s32[64,2]{0,1:T(2,128)S(1)}, s32[64,2]{0,1:T(2,128)}, u32[]{:S(2)}) copy-start(s32[64,2]{0,1:T(2,128)} %param.10) | copy-start | bytes 1540
  7.8 5.9 %collective-permute-start.1 = (f32[64,1024]{1,0:T(8,128)S(1)}, f32[64,1024]{1,0:T(8,128)S(1)}, u32[]{:S(2)}, u32[]{:S(2)}) collective-permute-start(f32[64,1024]{1,0:T(8,128)S(1)} %lending.1.lent), channel_id=1, source_target_pairs={{1,0},{2,1},{3,2},{4,3},{5,4},{6,5},{7,6},{8,7},{9,8},{10,9},{11,1... | collective-permute-start | bytes 786440 | tf_op jit(solution)/shard_map/ppermute | solution.py:372
  9.5 17.4 %copy-start = (s32[1024,4]{0,1:T(4,128)S(1)}, s32[1024,4]{0,1:T(4,128)}, u32[]{:S(2)}) copy-start(s32[1024,4]{0,1:T(4,128)} %param.11) | copy-start | bytes 49156
  13.7 4.9 %collective-permute-start.2 = (bf16[16,1024]{1,0:T(8,128)(2,1)S(1)}, bf16[16,1024]{1,0:T(8,128)(2,1)S(1)}, u32[]{:S(2)}, u32[]{:S(2)}) collective-permute-start(bf16[16,1024]{1,0:T(8,128)(2,1)S(1)} %get-tuple-element.24), channel_id=1, source_target_pairs={{0,8},{1,9},{2,10},{3,11},{4,12},{5,13},{6,14},{7,15},{8,0},{9,1},... | collective-permute-start | bytes 98312 | tf_op jit(solution)/shard_map/ppermute | solution.py:377
  15.0 5.8 %collective-permute-start.3 = (bf16[16,1024]{1,0:T(8,128)(2,1)S(1)}, bf16[16,1024]{1,0:T(8,128)(2,1)S(1)}, u32[]{:S(2)}, u32[]{:S(2)}) collective-permute-start(bf16[16,1024]{1,0:T(8,128)(2,1)S(1)} %get-tuple-element.25), channel_id=1, source_target_pairs={{0,12},{1,13},{2,14},{3,15},{4,8},{5,9},{6,10},{7,11},{8,4},{9,5},... | collective-permute-start | bytes 98312 | tf_op jit(solution)/shard_map/ppermute | solution.py:377
  16.4 4.5 %collective-permute-start.4 = (bf16[16,1024]{1,0:T(8,128)(2,1)S(1)}, bf16[16,1024]{1,0:T(8,128)(2,1)S(1)}, u32[]{:S(2)}, u32[]{:S(2)}) collective-permute-start(bf16[16,1024]{1,0:T(8,128)(2,1)S(1)} %get-tuple-element.26), channel_id=1, source_target_pairs={{0,4},{1,5},{2,6},{3,7},{4,0},{5,1},{6,2},{7,3},{8,12},{9,13},{10,... | collective-permute-start | bytes 98312 | tf_op jit(solution)/shard_map/ppermute | solution.py:377
  20.9 6.3 %collective-permute-start.7 = (bf16[64,1024]{1,0:T(8,128)(2,1)S(1)}, bf16[64,1024]{1,0:T(8,128)(2,1)S(1)}, u32[]{:S(2)}, u32[]{:S(2)}) collective-permute-start(bf16[64,1024]{1,0:T(8,128)(2,1)S(1)} %pad_maximum_fusion), channel_id=1, source_target_pairs={{0,1},{1,0},{2,3},{3,2},{4,5},{5,4},{6,7},{7,6},{8,9},{9,8},{10,11... | collective-permute-start | bytes 393224 | tf_op jit(solution)/shard_map/ppermute | solution.py:377
  21.0 5.0 %collective-permute-start.6 = (bf16[32,1024]{1,0:T(8,128)(2,1)S(1)}, bf16[32,1024]{1,0:T(8,128)(2,1)S(1)}, u32[]{:S(2)}, u32[]{:S(2)}) collective-permute-start(bf16[32,1024]{1,0:T(8,128)(2,1)S(1)} %constant_dynamic-update-slice_fusion.2.refs_1_), channel_id=1, source_target_pairs={{0,2},{1,3},{2,0},{3,1},{4,6},{5,7},{6,4},{7,5},{8,10},{9,11},{10,... | collective-permute-start | bytes 196616 | tf_op jit(solution)/shard_map/ppermute | solution.py:377
  22.4 4.5 %collective-permute-start.5 = (bf16[32,1024]{1,0:T(8,128)(2,1)S(1)}, bf16[32,1024]{1,0:T(8,128)(2,1)S(1)}, u32[]{:S(2)}, u32[]{:S(2)}) collective-permute-start(bf16[32,1024]{1,0:T(8,128)(2,1)S(1)} %constant_dynamic-update-slice_fusion.refs_0_), channel_id=1, source_target_pairs={{0,2},{1,3},{2,0},{3,1},{4,6},{5,7},{6,4},{7,5},{8,10},{9,11},{10,... | collective-permute-start | bytes 196616 | tf_op jit(solution)/shard_map/ppermute | solution.py:377
  26.0 1.3 %collective-permute-start.9 = (bf16[32,1024]{1,0:T(8,128)(2,1)S(1)}, bf16[32,1024]{1,0:T(8,128)(2,1)S(1)}, u32[]{:S(2)}, u32[]{:S(2)}) collective-permute-start(bf16[32,1024]{1,0:T(8,128)(2,1)S(1)} %collective-permute-done.6.refs_3_), channel_id=1, source_target_pairs={{0,1},{1,0},{2,3},{3,2},{4,5},{5,4},{6,7},{7,6},{8,9},{9,8},{10,11... | collective-permute-start | bytes 196616 | tf_op jit(solution)/shard_map/ppermute | solution.py:377
  26.9 1.3 %collective-permute-start.8 = (bf16[32,1024]{1,0:T(8,128)(2,1)S(1)}, bf16[32,1024]{1,0:T(8,128)(2,1)S(1)}, u32[]{:S(2)}, u32[]{:S(2)}) collective-permute-start(bf16[32,1024]{1,0:T(8,128)(2,1)S(1)} %collective-permute-done.5.refs_2_), channel_id=1, source_target_pairs={{0,1},{1,0},{2,3},{3,2},{4,5},{5,4},{6,7},{7,6},{8,9},{9,8},{10,11... | collective-permute-start | bytes 196616 | tf_op jit(solution)/shard_map/ppermute | solution.py:377
